TPU v7x, 32 devices: a whole 2x2x4 slice. The times are simulated.
32 devices in a mesh: src: 4 (over y, x), tgt: 8 (over z, core).
Axes of the slice: x: 2, y: 2, z: 4, core: 2. Of those that a mesh axis runs over, the one named last changes fastest.
Arguments:
- source_values: float32 [16, 65536], P(None, ('src', 'tgt')), may hold values from -6 to 6
- source_phase: float32 [65536], P(('src', 'tgt')), may hold values from -3.140625 to 3.140625
- leaf_interp: bfloat16 [64, 64], replicated, may hold values from -0.75 to 0.75
- level_interp: bfloat16 [11, 2, 64, 64], replicated, may hold values from -0.5 to 0.5
- level_phase: float32 [11, 3, 1024, 64], P(None, None, ('src', 'tgt')), may hold values from -3.140625 to 3.140625
- middle_interp: bfloat16 [64, 64], replicated, may hold values from -0.75 to 0.75
- middle_phase: float32 [2, 1024, 64], P(None, ('src', 'tgt')), may hold values from -3.140625 to 3.140625
- final_phase: float32 [1024, 64], P(('src', 'tgt')), may hold values from -3.140625 to 3.140625
- final_interp: bfloat16 [64, 64], replicated, may hold values from -0.75 to 0.75
- target_phase: float32 [65536], P(('src', 'tgt')), may hold values from -3.140625 to 3.140625
Outputs:
- target_values: float32 [2, 16, 65536], P(None, None, ('src', 'tgt'))
All inputs are finite; a program needn't handle non-finite values.
Results may differ from a plain program's by a relative error of at most 0.024.
Values may be sent and summed in bfloat16 or wider, within the bound.
A program may use at most 64 MiB of HBM per device.

v0:
```python
import functools

import jax
import jax.numpy as jnp
from jax import lax
from jax.experimental import pallas as pl
from jax.experimental.pallas import tpu as pltpu
from jax.sharding import PartitionSpec as P

LOCAL_SRC = 3
LOCAL_TGT = 3
MESH = pl.DeviceIdType.MESH
GROUP = 2
VLIM = 67043328
F32 = jnp.float32
BF16 = jnp.bfloat16

PI_HI = 3.140625
PI_LO = 9.67653589793e-4
SIN_C = (2.605166276178326e-06, -0.00019809046357444052, 0.008333050617328575, -0.16666657969904702, 0.9999999957158396)
COS_C = (-2.605107617861078e-07, 2.4760135505794177e-05, -0.0013888360842290288, 0.04166663620890442, -0.49999999356955516, 0.9999999997799034)


def cos_sin(x):
    k = lax.round(x * (1.0 / 3.141592653589793), lax.RoundingMethod.TO_NEAREST_EVEN)
    r = (x - k * PI_HI) - k * PI_LO
    z = r * r
    c = jnp.full_like(z, COS_C[0])
    for a in COS_C[1:]:
        c = c * z + a
    s = jnp.full_like(z, SIN_C[0])
    for a in SIN_C[1:]:
        s = s * z + a
    s = s * r
    half = k * 0.5
    odd = jnp.abs(half - lax.round(half, lax.RoundingMethod.TO_NEAREST_EVEN))
    sign = 1.0 - 4.0 * odd
    return c * sign, s * sign


def lane_low(shape, half):
    return lax.broadcasted_iota(jnp.int32, shape, len(shape) - 1) < half


def dup(x):
    return jnp.concatenate([x, x], -1)


def dup_halves(x, half):
    y = pltpu.roll(x, half, x.ndim - 1)
    low = lane_low(x.shape, half)
    return jnp.where(low, x, y), jnp.where(low, y, x)


def xor_rows(x, h):
    rows = x.shape[0]
    up = pltpu.roll(x, rows - h, 0)
    down = pltpu.roll(x, h, 0)
    row = lax.broadcasted_iota(jnp.int32, x.shape, 0)
    return jnp.where((row // h) % 2 == 0, up, down)


def xor_lead(x, h):
    return jnp.concatenate([x[i ^ h : (i ^ h) + 1] for i in range(x.shape[0])], 0)


def xor_index(i, j, size):
    bit = 1
    res = i
    while bit < size:
        if j & bit:
            res = res + bit * (1 - 2 * lax.rem(i // bit, 2))
        bit *= 2
    return res


def kernel(
    S, T, levels, src_bits, tgt_bits,
    values_h, sphase_h, leaf_h, lint_h, lphase_h, mint_h, mphase_h, fphase_h, fint_h, tphase_h,
    out,
    values, sphase, leaf, lint, lphase, mint, mphase, fphase, fint, tphase, obuf, in_sem, out_sem,
    w, wl, wm, wf, tc, ts, ph_src, pk2, pk, ph_tgt, send1, recv1, xa, xb, send2, recv2,
    ps_send, ps_recv, pt_send, pt_recv, c1_send, c1_recv, c2_send, c2_recv,
):
    s_me = lax.axis_index("src")
    t_me = lax.axis_index("tgt")
    half = leaf.shape[1]
    span = T * half
    R = S * T
    rhs = values.shape[0]
    rows = T * rhs
    K = LOCAL_SRC + src_bits
    M = K + tgt_bits
    N = levels

    barrier = pltpu.get_barrier_semaphore()
    for j in range(1, S):
        pl.semaphore_signal(barrier, inc=1, device_id=(lax.rem(s_me + j, S), t_me), device_id_type=MESH)
    for j in range(1, T):
        pl.semaphore_signal(barrier, inc=1, device_id=(s_me, lax.rem(t_me + j, T)), device_id_type=MESH)

    loads = [
        pltpu.make_async_copy(a, b, in_sem.at[i])
        for i, (a, b) in enumerate(
            (
                (sphase_h, sphase), (lphase_h, lphase), (leaf_h, leaf), (values_h, values),
                (lint_h, lint), (mphase_h, mphase), (fphase_h, fphase), (tphase_h, tphase),
                (mint_h, mint), (fint_h, fint),
            )
        )
    ]
    for load in loads:
        load.start()
    for load in loads[:3]:
        load.wait()

    sgn = jnp.where(lane_low((R, 2 * half), half), -1.0, 1.0)

    def put(idx, angle):
        c, s = cos_sin(angle * sgn)
        tc[idx] = c
        ts[idx] = s

    def put_level(n, prev, own, other, h):
        oth = xor_rows(other, h)
        put(2 * n, own if prev is None else prev + own)
        put(2 * n + 1, oth if prev is None else prev + oth)

    def lp(n, q):
        return dup(lphase[n, q])

    I_SEND1, I_MID, I_SEND2, I_FIN, I_TGT, I_SRC = (2 * N + i for i in range(6))

    low16 = lane_low((sphase.shape[0], 2 * half), half)

    def point_rows(ref):
        lo, hi = dup_halves(ref[...], half)
        n = lo.shape[0]
        return jnp.concatenate([jnp.concatenate([lo[i : i + 1], hi[i : i + 1]], 0) for i in range(n)], 0)

    c, s = cos_sin(point_rows(sphase))
    tc[I_SRC] = jnp.where(lane_low(c.shape, half), c, -s)
    for n in range(LOCAL_SRC):
        put_level(n, None if n == 0 else lp(n - 1, 2), lp(n, 0), lp(n, 1), 2**n)
    put(I_SEND1, lp(LOCAL_SRC - 1, 2))

    def fill(dst, r, L):
        z = jnp.zeros_like(L)
        lz = jnp.concatenate([L, z], 1)
        zl = jnp.concatenate([z, L], 1)
        wd = 2 * half
        dst[r : r + half, 0:wd] = lz
        dst[r : r + half, wd : 2 * wd] = zl
        dst[r + half : r + wd, 0:wd] = zl
        dst[r + half : r + wd, wd : 2 * wd] = lz

    fill(wl, 0, leaf[...])
    loads[4].wait()
    for n in range(LOCAL_SRC):
        fill(w.at[n], 0, lint[n, 0])
        fill(w.at[n], 2 * half, lint[n, 1])

    def blk(i):
        return pl.ds(pl.multiple_of(i * T, T), T)

    def ps_copy(j):
        e = xor_index(s_me, j, S)
        return pltpu.make_async_remote_copy(
            src_ref=lphase.at[pl.ds(LOCAL_SRC, src_bits), :, blk(e), :],
            dst_ref=ph_src.at[:, :, blk(s_me), :],
            send_sem=ps_send.at[j], recv_sem=ps_recv.at[j],
            device_id=(e, t_me), device_id_type=MESH,
        )

    def pt_copy(j):
        e = xor_index(t_me, j, T)
        return pltpu.make_async_remote_copy(
            src_ref=pk.at[pl.ds(pl.multiple_of(e * RP, 8), RP), :],
            dst_ref=ph_tgt.at[pl.ds(pl.multiple_of(t_me * RP, 8), RP), :],
            send_sem=pt_send.at[j], recv_sem=pt_recv.at[j],
            device_id=(s_me, e), device_id_type=MESH,
        )

    def tab(idx, i):
        return tc[idx, blk(i), :][:, None, :], ts[idx, blk(i), :][:, None, :]

    wd = 2 * half

    def split(y):
        y = y.reshape(T, rhs, 2 * wd)
        return y[:, :, :wd], y[:, :, wd:]

    def rot(v, sw, idx, i):
        c, s = tab(idx, i)
        return v * c + sw * s

    def dot(x, m):
        return jnp.dot(x, m, preferred_element_type=F32)

    def step(v, sw, n, i, h):
        own = rot(v, sw, 2 * n, i).astype(BF16)
        oth = xor_lead(rot(v, sw, 2 * n + 1, i), h).astype(BF16)
        x = jnp.concatenate([own, oth], -1).reshape(rows, 2 * wd)
        return split(dot(x, w[n]))

    def c1_copy(j):
        e = xor_index(s_me, j, S)
        return pltpu.make_async_remote_copy(
            src_ref=send1.at[e], dst_ref=recv1.at[s_me],
            send_sem=c1_send.at[j], recv_sem=c1_recv.at[j],
            device_id=(e, t_me), device_id_type=MESH,
        )

    loads[3].wait()
    state = []
    for e in range(S):
        parts = []
        for p in range(T // 2):
            parts.extend(dup_halves(values[:, e * span + p * wd : e * span + (p + 1) * wd], half))
        x = jnp.stack(parts, 0) * tc[I_SRC, blk(e), :][:, None, :]
        state.append(split(dot(x.astype(BF16).reshape(rows, wd), wl[...])))
    for n in range(LOCAL_SRC):
        state = [step(v, sw, n, e, 2**n) for e, (v, sw) in enumerate(state)]
    for e, (v, sw) in enumerate(state):
        send1[e] = rot(v, sw, I_SEND1, e).astype(BF16)

    loads[5].wait()
    def arr(q):
        if q < 2:
            return mphase[q]
        return lphase[K + (q - 2) // 3, (q - 2) % 3]

    nq = 2 + 3 * tgt_bits
    Q = (nq + 1) // 2
    RP = pk.shape[0] // T
    for q in range(Q):
        a = arr(2 * q)
        b = arr(2 * q + 1) if 2 * q + 1 < nq else a
        pk2[q * R : (q + 1) * R, :] = jnp.concatenate([a, b], -1)
    for d in range(T):
        pk[d * RP : d * RP + Q * S, :] = pk2[pl.ds(d, Q * S, stride=T), :]

    pl.semaphore_wait(barrier, S - 1 + T - 1)
    for j in range(S - 1, 0, -1):
        ps_copy(j).start()
    for j in range(T - 1, 0, -1):
        pt_copy(j).start()

    for j in range(S - 1, 0, -1):
        c1_copy(j).start()
    recv1[s_me] = send1[s_me]

    for load in loads[6:]:
        load.wait()
    for n in range(LOCAL_SRC, N):
        fill(w.at[n], 0, lint[n, 0])
        fill(w.at[n], 2 * half, lint[n, 1])
    fill(wm, 0, mint[...])
    fill(wf, 0, fint[...])

    ph_src[:, :, blk(s_me), :] = lphase[LOCAL_SRC:K, :, blk(s_me), :]
    own_rows = pl.ds(pl.multiple_of(t_me * RP, 8), RP)
    ph_tgt[own_rows, :] = pk[own_rows, :]

    for n in range(M, N):
        put_level(n, None if n == M else lp(n - 1, 2), lp(n, 0), lp(n, 1), 2 ** (n - M))
    put(I_FIN, lp(N - 1, 2) + dup(fphase[...]))
    put(I_TGT, point_rows(tphase))

    for j in range(1, S):
        ps_copy(j).wait()
    for b in range(src_bits):
        n = LOCAL_SRC + b
        prev = None if b == 0 else dup(ph_src[b - 1, 2])
        put_level(n, prev, dup(ph_src[b, 0]), dup(ph_src[b, 1]), T * 2**b)

    for j in range(1, T):
        pt_copy(j).wait()
    ang = []
    for q in range(Q):
        packed = jnp.concatenate(
            [ph_tgt[pl.ds(q * S + i, T, stride=RP), :] for i in range(S)], 0
        )
        ang.extend(dup_halves(packed, half))
    put(I_MID, dup(ph_src[src_bits - 1, 2]) + ang[0])
    for b in range(tgt_bits):
        n = K + b
        prev = ang[1] if b == 0 else ang[2 + 3 * (b - 1) + 2]
        put_level(n, prev, ang[2 + 3 * b], ang[2 + 3 * b + 1], 2**b)
    put(I_SEND2, ang[2 + 3 * (tgt_bits - 1) + 2])

    for j in range(1, S):
        c1_copy(j).wait()

    bufs = (xa, xb)
    for b in range(src_bits):
        n = LOCAL_SRC + b
        dst = bufs[b % 2]
        for i in range(S):
            if b == 0:
                v = recv1[i].astype(F32)
                sw = pltpu.roll(v, half, 2)
            else:
                v, sw = split(dot(bufs[(b - 1) % 2][i], w[n - 1]))
            own = rot(v, sw, 2 * n, i).astype(BF16)
            oth = rot(v, sw, 2 * n + 1, i).astype(BF16)
            dst[i, :, :wd] = own.reshape(rows, wd)
            dst[i ^ 2**b, :, wd:] = oth.reshape(rows, wd)

    def c2_copy(i, j):
        e = xor_index(t_me, j, T)
        return pltpu.make_async_remote_copy(
            src_ref=send2.at[i, e], dst_ref=recv2.at[i, t_me],
            send_sem=c2_send.at[i, j], recv_sem=c2_recv.at[i, j],
            device_id=(s_me, e), device_id_type=MESH,
        )

    for g in range(0, S, GROUP):
        blocks = range(g, min(g + GROUP, S))
        state = [split(dot(bufs[(src_bits - 1) % 2][i], w[K - 1])) for i in blocks]
        state = [rot(v, sw, I_MID, i).astype(BF16).reshape(rows, wd) for i, (v, sw) in zip(blocks, state)]
        state = [split(dot(x, wm[...])) for x in state]
        for b in range(tgt_bits):
            state = [step(v, sw, K + b, i, 2**b) for i, (v, sw) in zip(blocks, state)]
        for i, (v, sw) in zip(blocks, state):
            send2[i] = rot(v, sw, I_SEND2, i).astype(BF16)
        for i in blocks:
            for j in range(T - 1, 0, -1):
                c2_copy(i, j).start()
            recv2[i, t_me] = send2[i, t_me]

    low3 = lane_low((rhs, wd), half)

    def o_copy(i):
        cols = pl.ds(i * span, span)
        return pltpu.make_async_copy(obuf.at[:, :, cols], out.at[:, :, cols], out_sem.at[i])

    for g in range(0, S, GROUP):
        blocks = range(g, min(g + GROUP, S))
        for i in blocks:
            for j in range(1, T):
                c2_copy(i, j).wait()
        state = []
        for i in blocks:
            v = recv2[i].astype(F32)
            state.append((v, pltpu.roll(v, half, 2)))
        for n in range(M, N):
            state = [step(v, sw, n, i, 2 ** (n - M)) for i, (v, sw) in zip(blocks, state)]
        state = [rot(v, sw, I_FIN, i).astype(BF16).reshape(rows, wd) for i, (v, sw) in zip(blocks, state)]
        state = [split(dot(x, wf[...])) for x in state]
        for i, (v, sw) in zip(blocks, state):
            r = rot(v, sw, I_TGT, i)
            rr = pltpu.roll(r, half, 2)
            for p in range(T // 2):
                col = pl.ds(i * T * half + p * wd, wd)
                obuf[0, :, col] = jnp.where(low3, r[2 * p], rr[2 * p + 1])
                obuf[1, :, col] = jnp.where(low3, rr[2 * p], r[2 * p + 1])
            o_copy(i).start()
    for i in range(S):
        o_copy(i).wait()


def shards(
    source_values, source_phase, leaf_interp, level_interp, level_phase,
    middle_interp, middle_phase, final_phase, final_interp, target_phase,
):
    S = lax.axis_size("src")
    T = lax.axis_size("tgt")
    R = level_phase.shape[2]
    assert R == S * T
    rhs = source_values.shape[0]
    half = leaf_interp.shape[1]
    wd = 2 * half
    N = level_phase.shape[0]
    src_bits = S.bit_length() - 1
    tgt_bits = T.bit_length() - 1
    assert N == LOCAL_SRC + src_bits + tgt_bits + LOCAL_TGT
    Q = (2 + 3 * tgt_bits + 1) // 2
    RP = -(-Q * S // 8) * 8
    ntab = 2 * N + 6
    vm = pltpu.VMEM
    dma = pltpu.SemaphoreType.DMA
    args = (
        source_values, source_phase.reshape(-1, wd), leaf_interp, level_interp, level_phase,
        middle_interp, middle_phase, final_phase, final_interp, target_phase.reshape(-1, wd),
    )
    return pl.pallas_call(
        functools.partial(kernel, S, T, N, src_bits, tgt_bits),
        out_shape=jax.ShapeDtypeStruct((2,) + source_values.shape, F32),
        in_specs=[pl.BlockSpec(memory_space=pltpu.HBM)] * 10,
        out_specs=pl.BlockSpec(memory_space=pl.ANY),
        scratch_shapes=[vm(a.shape, a.dtype) for a in args] + [
            vm((2,) + source_values.shape, F32), dma((10,)), dma((S,)),
            vm((N, 2 * wd, 2 * wd), BF16), vm((wd, 2 * wd), BF16),
            vm((wd, 2 * wd), BF16), vm((wd, 2 * wd), BF16),
            vm((ntab, R, wd), F32), vm((ntab, R, wd), F32),
            vm((src_bits, 3, R, half), F32), vm((Q * R, wd), F32),
            vm((T * RP, wd), F32), vm((T * RP, wd), F32),
            vm((S, T, rhs, wd), BF16), vm((S, T, rhs, wd), BF16),
            vm((S, T * rhs, 2 * wd), BF16), vm((S, T * rhs, 2 * wd), BF16),
            vm((S, T, rhs, wd), BF16), vm((S, T, rhs, wd), BF16),
            dma((S,)), dma((S,)), dma((T,)), dma((T,)),
            dma((S,)), dma((S,)), dma((S, T)), dma((S, T)),
        ],
        compiler_params=pltpu.CompilerParams(
            collective_id=0, has_side_effects=True, vmem_limit_bytes=VLIM
        ),
    )(*args)


def solution(mesh):
    return jax.shard_map(
        shards,
        mesh=mesh,
        in_specs=(
            P(None, ("src", "tgt")),
            P(("src", "tgt")),
            P(),
            P(),
            P(None, None, ("src", "tgt"), None),
            P(),
            P(None, ("src", "tgt"), None),
            P(("src", "tgt"), None),
            P(),
            P(("src", "tgt")),
        ),
        out_specs=P(None, None, ("src", "tgt")),
        check_vma=False,
    )
```

profile of v0, /device:TPU:0, one launch (start us, length us, event | category | flops | bytes accessed | tf_op | source)
XLA Modules:
  0.0 20.4 jit_solution(5762111002783871036)
XLA Ops:
  0.0 18.7 %shard_map.100 = f32[2,16,2048]{2,1,0:T(8,128)} custom-call(f32[16,2048]{1,0:T(8,128)} %values_h.1, f32[16,128]{1,0:T(8,128)} %bitcast.2, bf16[64,64]{1,0:T(8,128)(2,1)} %leaf_h.1, bf16[11,2,64,64]{3,2,1,0:T(8,128)(2,1)} %lint_h.1, f32[11,3,32,64]{3,2,1,0:T(8,128)} %lphase_h.1, bf16[64,64]{1,0:T(8,128)(2,1)} %mint_h.1, f32[2,32,64]{2,1,0:T(8,128)} %mphase_h.1, ...), custom_call_target="tpu_custom_call" | custom-call | tf_op jit(solution)/shard_map/pallas_call | solution.py:387
  18.7 1.7 %copy.12 = f32[2,16,2048]{2,1,0:T(8,128)} copy(f32[2,16,2048]{2,1,0:T(8,128)} %shard_map.100) | data formatting | bytes 524288
where the time goes:
time: 20.6 us; the launch traced here: 20.4 us
  Pallas kernels  18.7 us (91%)
  local copies, waits for them, and re-layouts  1.67 us (8%)
    pallas_call x1, Pallas kernels, shards(): pl.pallas_call(functools.partial(kernel, S, T, N, src_bits, tgt_bits), ou...  18.7 us
    unnamed x1, local copies, waits for them, and re-layouts  1.67 us

commit v1 on v0

v1 whole, which is shorter than its diff:
```python
import functools

import jax
import jax.numpy as jnp
from jax import lax
from jax.experimental import pallas as pl
from jax.experimental.pallas import tpu as pltpu
from jax.sharding import PartitionSpec as P

LOCAL_SRC = 3
LOCAL_TGT = 3
MESH = pl.DeviceIdType.MESH
SRC_GROUPS = (2, 2)
MID_GROUPS = (2, 2)
FIN_GROUPS = (2, 2)
VLIM = 40 * 1024 * 1024
F32 = jnp.float32
BF16 = jnp.bfloat16

PI_HI = 3.140625
PI_LO = 9.67653589793e-4
SIN_C = (2.605166276178326e-06, -0.00019809046357444052, 0.008333050617328575, -0.16666657969904702, 0.9999999957158396)
COS_C = (-2.605107617861078e-07, 2.4760135505794177e-05, -0.0013888360842290288, 0.04166663620890442, -0.49999999356955516, 0.9999999997799034)


def cos_sin(x):
    k = lax.round(x * (1.0 / 3.141592653589793), lax.RoundingMethod.TO_NEAREST_EVEN)
    r = (x - k * PI_HI) - k * PI_LO
    z = r * r
    c = jnp.full_like(z, COS_C[0])
    for a in COS_C[1:]:
        c = c * z + a
    s = jnp.full_like(z, SIN_C[0])
    for a in SIN_C[1:]:
        s = s * z + a
    s = s * r
    half = k * 0.5
    odd = jnp.abs(half - lax.round(half, lax.RoundingMethod.TO_NEAREST_EVEN))
    sign = 1.0 - 4.0 * odd
    return c * sign, s * sign


def lane_low(shape, half):
    return lax.broadcasted_iota(jnp.int32, shape, len(shape) - 1) < half


def dup(x):
    return jnp.concatenate([x, x], -1)


def dup_halves(x, half):
    y = pltpu.roll(x, half, x.ndim - 1)
    low = lane_low(x.shape, half)
    return jnp.where(low, x, y), jnp.where(low, y, x)


def xor_rows(x, h):
    rows = x.shape[0]
    up = pltpu.roll(x, rows - h, 0)
    down = pltpu.roll(x, h, 0)
    row = lax.broadcasted_iota(jnp.int32, x.shape, 0)
    return jnp.where((row // h) % 2 == 0, up, down)


def xor_lead(x, h):
    return jnp.concatenate([x[i ^ h : (i ^ h) + 1] for i in range(x.shape[0])], 0)


def xor_index(i, j, size):
    bit = 1
    res = i
    while bit < size:
        if j & bit:
            res = res + bit * (1 - 2 * lax.rem(i // bit, 2))
        bit *= 2
    return res


def groups_of(n, sizes):
    at, res = 0, []
    for k in sizes:
        if at < n:
            res.append(tuple(range(at, min(at + k, n))))
            at += k
    while at < n:
        res.append(tuple(range(at, min(at + sizes[-1], n))))
        at += sizes[-1]
    return res


def kernel(
    S, T, levels, src_bits, tgt_bits,
    values_h, sphase_h, leaf_h, lint_h, lphase_h, mint_h, mphase_h, fphase_h, fint_h, tphase_h,
    out,
    values, sphase, leaf, lint, lphase, mint, mphase, fphase, fint, tphase, in_sem,
    w, wl, wm, wf, tc, ts, ps_out, ph_src, pk2, pk, ph_tgt, send1, xa, xb, send2, recv2,
    ps_send, ps_recv, pt_send, pt_recv, c1_send, c1_recv, c2_send, c2_recv,
):
    s_me = lax.axis_index("src")
    t_me = lax.axis_index("tgt")
    half = leaf.shape[1]
    wd = 2 * half
    span = T * half
    R = S * T
    rhs = values.shape[0]
    rows = T * rhs
    K = LOCAL_SRC + src_bits
    M = K + tgt_bits
    N = levels

    barrier = pltpu.get_barrier_semaphore()
    for j in range(1, T):
        pl.semaphore_signal(barrier, inc=1, device_id=(s_me, lax.rem(t_me + j, T)), device_id_type=MESH)
    for j in range(1, S):
        pl.semaphore_signal(barrier, inc=1, device_id=(lax.rem(s_me + j, S), t_me), device_id_type=MESH)

    near = LOCAL_SRC + 1
    loads = [
        pltpu.make_async_copy(a, b, in_sem.at[i])
        for i, (a, b) in enumerate(
            (
                (sphase_h, sphase), (lphase_h.at[0:near], lphase.at[0:near]), (leaf_h, leaf),
                (lint_h.at[0:LOCAL_SRC], lint.at[0:LOCAL_SRC]), (values_h, values),
                (lphase_h.at[near:N], lphase.at[near:N]), (mphase_h, mphase),
                (lint_h.at[LOCAL_SRC:N], lint.at[LOCAL_SRC:N]),
                (fphase_h, fphase), (tphase_h, tphase), (mint_h, mint), (fint_h, fint),
            )
        )
    ]
    for load in loads:
        load.start()

    sgn = jnp.where(lane_low((R, wd), half), -1.0, 1.0)

    def put(idx, angle):
        c, s = cos_sin(angle * sgn)
        tc[idx] = c
        ts[idx] = s

    def put_level(n, prev, own, other, h):
        oth = xor_rows(other, h)
        put(2 * n, own if prev is None else prev + own)
        put(2 * n + 1, oth if prev is None else prev + oth)

    def lp(n, q):
        return dup(lphase[n, q])

    I_SEND1, I_MID, I_FIN, I_TGT, I_SRC = (2 * N + i for i in range(5))

    def point_rows(ref):
        lo, hi = dup_halves(ref[...], half)
        n = lo.shape[0]
        return jnp.concatenate([jnp.concatenate([lo[i : i + 1], hi[i : i + 1]], 0) for i in range(n)], 0)

    def fill(dst, r, L):
        z = jnp.zeros_like(L)
        lz = jnp.concatenate([L, z], 1)
        zl = jnp.concatenate([z, L], 1)
        dst[r : r + half, 0:wd] = lz
        dst[r : r + half, wd : 2 * wd] = zl
        dst[r + half : r + wd, 0:wd] = zl
        dst[r + half : r + wd, wd : 2 * wd] = lz

    def blk(i):
        return pl.ds(pl.multiple_of(i * T, T), T)

    def ps_copy(j):
        e = xor_index(s_me, j, S)
        return pltpu.make_async_remote_copy(
            src_ref=ps_out.at[:, blk(e), :], dst_ref=ph_src.at[:, blk(s_me), :],
            send_sem=ps_send, recv_sem=ps_recv, device_id=(e, t_me), device_id_type=MESH,
        )

    def pt_copy(j):
        e = xor_index(t_me, j, T)
        return pltpu.make_async_remote_copy(
            src_ref=pk.at[e], dst_ref=ph_tgt.at[t_me],
            send_sem=pt_send, recv_sem=pt_recv, device_id=(s_me, e), device_id_type=MESH,
        )

    def c1_copy(j):
        e = xor_index(s_me, j, S)
        return pltpu.make_async_remote_copy(
            src_ref=send1.at[j], dst_ref=xa.at[s_me, :, pl.ds(0, wd)],
            send_sem=c1_send, recv_sem=c1_recv, device_id=(e, t_me), device_id_type=MESH,
        )

    def c2_copy(i, j):
        e = xor_index(t_me, j, T)
        return pltpu.make_async_remote_copy(
            src_ref=send2.at[i, e], dst_ref=recv2.at[i, t_me],
            send_sem=c2_send, recv_sem=c2_recv.at[i], device_id=(s_me, e), device_id_type=MESH,
        )

    s_one = (xor_index(s_me, 1, S), t_me)
    t_one = (s_me, xor_index(t_me, 1, T))
    ps_all = pltpu.make_async_remote_copy(
        src_ref=ps_out.at[:, pl.ds(0, R - T), :], dst_ref=ph_src.at[:, pl.ds(0, R - T), :],
        send_sem=ps_send, recv_sem=ps_recv, device_id=s_one, device_id_type=MESH,
    )
    pt_all = pltpu.make_async_remote_copy(
        src_ref=pk.at[pl.ds(0, T - 1)], dst_ref=ph_tgt.at[pl.ds(0, T - 1)],
        send_sem=pt_send, recv_sem=pt_recv, device_id=t_one, device_id_type=MESH,
    )
    c1_all = pltpu.make_async_remote_copy(
        src_ref=send1.at[pl.ds(0, S - 1)], dst_ref=xa.at[pl.ds(0, S - 1), :, pl.ds(0, wd)],
        send_sem=c1_send, recv_sem=c1_recv, device_id=s_one, device_id_type=MESH,
    )

    def c2_all(i, n):
        return pltpu.make_async_remote_copy(
            src_ref=send2.at[pl.ds(i, n), pl.ds(0, T - 1)], dst_ref=recv2.at[pl.ds(i, n), pl.ds(0, T - 1)],
            send_sem=c2_send, recv_sem=c2_recv.at[i], device_id=t_one, device_id_type=MESH,
        )

    def tab(idx, i):
        return tc[idx, blk(i), :][:, None, :], ts[idx, blk(i), :][:, None, :]

    def split(y):
        y = y.reshape(T, rhs, 2 * wd)
        return y[:, :, :wd], y[:, :, wd:]

    def rot(v, sw, idx, i):
        c, s = tab(idx, i)
        return v * c + sw * s

    def dot(x, m):
        return jnp.dot(x, m, preferred_element_type=F32)

    def step(v, sw, n, i, h):
        own = rot(v, sw, 2 * n, i).astype(BF16)
        oth = xor_lead(rot(v, sw, 2 * n + 1, i), h).astype(BF16)
        x = jnp.concatenate([own, oth], -1).reshape(rows, 2 * wd)
        return split(dot(x, w[n]))

    def last_step(v, sw, n, i, h):
        own = rot(v, sw, 2 * n, i).astype(BF16)
        oth = xor_lead(rot(v, sw, 2 * n + 1, i), h).astype(BF16)
        x = jnp.concatenate([own, oth], -1).reshape(rows, 2 * wd)
        return dot(x, w[n, :, :wd]).reshape(T, rhs, wd)

    for load in loads[:4]:
        load.wait()

    c, s = cos_sin(point_rows(sphase))
    tc[I_SRC] = jnp.where(lane_low(c.shape, half), c, -s)
    for n in range(LOCAL_SRC):
        put_level(n, None if n == 0 else lp(n - 1, 2), lp(n, 0), lp(n, 1), 2**n)
    put(I_SEND1, lp(LOCAL_SRC - 1, 2) + lp(LOCAL_SRC, 0))
    fill(wl, 0, leaf[...])
    for n in range(LOCAL_SRC):
        fill(w.at[n], 0, lint[n, 0])
        fill(w.at[n], 2 * half, lint[n, 1])

    def src_part(js):
        blocks = [xor_index(s_me, j, S) for j in js]
        state = []
        for e in blocks:
            at = pl.multiple_of(e * span, span)
            parts = []
            for p in range(T // 2):
                parts.extend(dup_halves(values[:, pl.ds(pl.multiple_of(at + p * wd, wd), wd)], half))
            x = jnp.stack(parts, 0) * tc[I_SRC, blk(e), :][:, None, :]
            state.append(split(dot(x.astype(BF16).reshape(rows, wd), wl[...])))
        for n in range(LOCAL_SRC):
            state = [step(v, sw, n, e, 2**n) for e, (v, sw) in zip(blocks, state)]
        for j, e, (v, sw) in zip(js, blocks, state):
            y = rot(v, sw, I_SEND1, e).astype(BF16).reshape(rows, wd)
            if j:
                send1[j] = y
            else:
                xa[s_me, :, :wd] = y

    def c1_start(js):
        for j in js:
            if j:
                c1_copy(j).start()

    for load in loads[4:7]:
        load.wait()

    def pick(arrays, q):
        a = arrays[2 * q]()
        b = arrays[2 * q + 1]() if 2 * q + 1 < len(arrays) else a
        return jnp.concatenate([a, b], -1)

    src_arrays = [functools.partial(lambda n, q: lphase[n, q], n, q) for n in range(LOCAL_SRC, K) for q in range(3)]
    for q in range(ps_out.shape[0]):
        ps_out[q] = pick(src_arrays, q)

    tgt_arrays = [functools.partial(lambda q: mphase[q], q) for q in range(2)]
    tgt_arrays += [functools.partial(lambda n, q: lphase[n, q], n, q) for n in range(K, M) for q in range(3)]
    tgt_arrays = tgt_arrays[:-1]
    Q = (len(tgt_arrays) + 1) // 2
    for q in range(Q):
        pk2[q * R : (q + 1) * R, :] = pick(tgt_arrays, q)
    for d in range(T):
        pk[d, 0 : Q * S, :] = pk2[pl.ds(d, Q * S, stride=T), :]

    order = [tuple(S - 1 - i for i in g) for g in groups_of(S, SRC_GROUPS)]
    src_part(order[0])
    pl.semaphore_wait(barrier, S - 1 + T - 1)
    for j in range(S - 1, 0, -1):
        ps_copy(j).start()
    c1_start(order[0])
    for j in range(T - 1, 0, -1):
        pt_copy(j).start()
    for js in order[1:]:
        src_part(js)
        c1_start(js)

    for load in loads[7:]:
        load.wait()
    for n in range(LOCAL_SRC, N):
        fill(w.at[n], 0, lint[n, 0])
        fill(w.at[n], 2 * half, lint[n, 1])
    fill(wm, 0, mint[...])
    fill(wf, 0, fint[...])

    ph_src[:, blk(s_me), :] = ps_out[:, blk(s_me), :]
    ph_tgt[t_me] = pk[t_me]

    for n in range(M, N):
        put_level(n, lp(n - 1, 2), lp(n, 0), lp(n, 1), 2 ** (n - M))
    put(I_FIN, lp(N - 1, 2) + dup(fphase[...]))
    put(I_TGT, point_rows(tphase))

    ps_all.wait_recv()
    sang = []
    for q in range(ps_out.shape[0]):
        sang.extend(dup_halves(ph_src[q], half))
    for b in range(src_bits):
        n = LOCAL_SRC + b
        if b == 0:
            put(2 * n + 1, xor_rows(sang[1], T) - sang[0])
        else:
            put_level(n, sang[3 * b - 1], sang[3 * b], sang[3 * b + 1], T * 2**b)

    pt_all.wait_recv()
    ang = []
    for q in range(Q):
        packed = jnp.concatenate([ph_tgt[:, q * S + i, :] for i in range(S)], 0)
        ang.extend(dup_halves(packed, half))
    put(I_MID, sang[3 * src_bits - 1] + ang[0])
    for b in range(tgt_bits):
        n = K + b
        put_level(n, ang[1] if b == 0 else ang[3 * b + 1], ang[3 * b + 2], ang[3 * b + 3], 2**b)

    c1_all.wait_recv()

    bufs = (xa, xb)
    for b in range(src_bits):
        n = LOCAL_SRC + b
        dst = bufs[b % 2]
        for i in range(S):
            if b == 0:
                v = xa[i, :, :wd].astype(F32).reshape(T, rhs, wd)
                sw = pltpu.roll(v, half, 2)
            else:
                v, sw = split(dot(bufs[(b - 1) % 2][i], w[n - 1]))
                dst[i, :, :wd] = rot(v, sw, 2 * n, i).astype(BF16).reshape(rows, wd)
            dst[i ^ 2**b, :, wd:] = rot(v, sw, 2 * n + 1, i).astype(BF16).reshape(rows, wd)

    for blocks in groups_of(S, MID_GROUPS):
        state = [split(dot(bufs[(src_bits - 1) % 2][i], w[K - 1])) for i in blocks]
        state = [rot(v, sw, I_MID, i).astype(BF16).reshape(rows, wd) for i, (v, sw) in zip(blocks, state)]
        state = [split(dot(x, wm[...])) for x in state]
        for b in range(tgt_bits):
            if b < tgt_bits - 1:
                state = [step(v, sw, K + b, i, 2**b) for i, (v, sw) in zip(blocks, state)]
            else:
                state = [last_step(v, sw, K + b, i, 2**b) for i, (v, sw) in zip(blocks, state)]
        for i, v in zip(blocks, state):
            send2[i] = v.astype(BF16)
        for i in blocks:
            for j in range(T - 1, 0, -1):
                c2_copy(i, j).start()
            recv2[i, t_me] = send2[i, t_me]

    low3 = lane_low((rhs, wd), half)

    for blocks in groups_of(S, FIN_GROUPS):
        for i in blocks:
            c2_all(i, 1).wait_recv()
        state = []
        for i in blocks:
            v = recv2[i].astype(F32)
            state.append((v, pltpu.roll(v, half, 2)))
        for n in range(M, N):
            state = [step(v, sw, n, i, 2 ** (n - M)) for i, (v, sw) in zip(blocks, state)]
        state = [rot(v, sw, I_FIN, i).astype(BF16).reshape(rows, wd) for i, (v, sw) in zip(blocks, state)]
        state = [split(dot(x, wf[...])) for x in state]
        for i, (v, sw) in zip(blocks, state):
            r = rot(v, sw, I_TGT, i)
            rr = pltpu.roll(r, half, 2)
            for p in range(T // 2):
                col = pl.ds(i * T * half + p * wd, wd)
                out[0, :, col] = jnp.where(low3, r[2 * p], rr[2 * p + 1])
                out[1, :, col] = jnp.where(low3, rr[2 * p], r[2 * p + 1])
    ps_all.wait_send()
    pt_all.wait_send()
    c1_all.wait_send()
    c2_all(0, S).wait_send()


def shards(
    source_values, source_phase, leaf_interp, level_interp, level_phase,
    middle_interp, middle_phase, final_phase, final_interp, target_phase,
):
    S = lax.axis_size("src")
    T = lax.axis_size("tgt")
    R = level_phase.shape[2]
    assert R == S * T
    rhs = source_values.shape[0]
    half = leaf_interp.shape[1]
    wd = 2 * half
    N = level_phase.shape[0]
    src_bits = S.bit_length() - 1
    tgt_bits = T.bit_length() - 1
    assert N == LOCAL_SRC + src_bits + tgt_bits + LOCAL_TGT
    Q1 = (3 * src_bits + 1) // 2
    Q = (1 + 3 * tgt_bits + 1) // 2
    ntab = 2 * N + 5
    vm = pltpu.VMEM
    dma = pltpu.SemaphoreType.DMA
    args = (
        source_values, source_phase.reshape(-1, wd), leaf_interp, level_interp, level_phase,
        middle_interp, middle_phase, final_phase, final_interp, target_phase.reshape(-1, wd),
    )
    return pl.pallas_call(
        functools.partial(kernel, S, T, N, src_bits, tgt_bits),
        out_shape=pltpu.VMEM((2,) + source_values.shape, F32),
        in_specs=[pl.BlockSpec(memory_space=pltpu.HBM)] * 10,
        out_specs=pl.BlockSpec(memory_space=pltpu.VMEM),
        scratch_shapes=[vm(a.shape, a.dtype) for a in args] + [
            dma((12,)),
            vm((N, 2 * wd, 2 * wd), BF16), vm((wd, 2 * wd), BF16),
            vm((wd, 2 * wd), BF16), vm((wd, 2 * wd), BF16),
            vm((ntab, R, wd), F32), vm((ntab, R, wd), F32),
            vm((Q1, R, wd), F32), vm((Q1, R, wd), F32), vm((Q * R, wd), F32),
            vm((T, Q * S, wd), F32), vm((T, Q * S, wd), F32),
            vm((S, T * rhs, wd), BF16),
            vm((S, T * rhs, 2 * wd), BF16), vm((S, T * rhs, 2 * wd), BF16),
            vm((S, T, rhs, wd), BF16), vm((S, T, rhs, wd), BF16),
            dma(()), dma(()), dma(()), dma(()),
            dma(()), dma(()), dma(()), dma((S,)),
        ],
        compiler_params=pltpu.CompilerParams(
            collective_id=0, has_side_effects=True, vmem_limit_bytes=VLIM
        ),
    )(*[pltpu.with_memory_space_constraint(a, pltpu.HBM) for a in args])


def solution(mesh):
    return jax.shard_map(
        shards,
        mesh=mesh,
        in_specs=(
            P(None, ("src", "tgt")),
            P(("src", "tgt")),
            P(),
            P(),
            P(None, None, ("src", "tgt"), None),
            P(),
            P(None, ("src", "tgt"), None),
            P(("src", "tgt"), None),
            P(),
            P(("src", "tgt")),
        ),
        out_specs=P(None, None, ("src", "tgt")),
        check_vma=False,
    )
```

time: 20.6 us -> 17.4 us (0.84)
  Pallas kernels: 18.7 us -> 16.5 us
  local copies, waits for them, and re-layouts: 1.67 us -> 0.71 us
    pallas_call x1, Pallas kernels: 18.7 us -> 16.5 us  [shards(): pl.pallas_call(functools.partial(kernel, S, T, N, src_bits, tgt_bits), ou...]
    unnamed x1, local copies, waits for them, and re-layouts: 1.67 us -> 0.71 us
where the time goes in v1:
time: 17.4 us; the launch traced here: 17.2 us
  Pallas kernels  16.5 us (95%)
  local copies, waits for them, and re-layouts  0.71 us (4%)
    pallas_call x1, Pallas kernels, shards(): pl.pallas_call(functools.partial(kernel, S, T, N, src_bits, tgt_bits), ou...  16.5 us
    unnamed x1, local copies, waits for them, and re-layouts  0.71 us

profile of v1, /device:TPU:0, one launch (start us, length us, event | category | flops | bytes accessed | tf_op | source)
XLA Modules:
  0.0 17.2 jit_solution(9221410141684384638)
XLA Ops:
  0.0 16.5 %shard_map.100 = f32[2,16,2048]{2,1,0:T(8,128)S(1)} custom-call(f32[16,2048]{1,0:T(8,128)} %values_h.1, f32[16,128]{1,0:T(8,128)} %bitcast.2, bf16[64,64]{1,0:T(8,128)(2,1)} %leaf_h.1, bf16[11,2,64,64]{3,2,1,0:T(8,128)(2,1)} %lint_h.1, f32[11,3,32,64]{3,2,1,0:T(8,128)} %lphase_h.1, bf16[64,64]{1,0:T(8,128)(2,1)} %mint_h.1, f32[2,32,64]{2,1,0:T(8,128)} %mphase_h.1, ...), custom_call_target="tpu_custom_call" | custom-call | tf_op jit(solution)/shard_map/pallas_call | solution.py:430
  16.5 0.7 %copy.12 = f32[2,16,2048]{2,1,0:T(8,128)} copy(f32[2,16,2048]{2,1,0:T(8,128)S(1)} %shard_map.100) | data formatting | bytes 524288

commit v2 on v1

--- a/solution.py
+++ b/solution.py
@@ -10,12 +10,13 @@
 LOCAL_SRC = 3
 LOCAL_TGT = 3
 MESH = pl.DeviceIdType.MESH
-SRC_GROUPS = (2, 2)
-MID_GROUPS = (2, 2)
-FIN_GROUPS = (2, 2)
+SRC_GROUPS = (4,)
+MID_GROUPS = (4,)
+FIN_GROUPS = (4,)
 VLIM = 40 * 1024 * 1024
 F32 = jnp.float32
 BF16 = jnp.bfloat16
+SENT = jnp.float32
 
 PI_HI = 3.140625
 PI_LO = 9.67653589793e-4
@@ -76,6 +77,14 @@
     return res
 
 
+def encode(x):
+    return x
+
+
+def decode(x):
+    return x
+
+
 def groups_of(n, sizes):
     at, res = 0, []
     for k in sizes:
@@ -88,12 +97,16 @@
     return res
 
 
+def pairs_of(refs):
+    return [(refs[i], refs[min(i + 1, len(refs) - 1)]) for i in range(0, len(refs), 2)]
+
+
 def kernel(
     S, T, levels, src_bits, tgt_bits,
     values_h, sphase_h, leaf_h, lint_h, lphase_h, mint_h, mphase_h, fphase_h, fint_h, tphase_h,
     out,
     values, sphase, leaf, lint, lphase, mint, mphase, fphase, fint, tphase, in_sem,
-    w, wl, wm, wf, tc, ts, ps_out, ph_src, pk2, pk, ph_tgt, send1, xa, xb, send2, recv2,
+    w, wl, wm, wf, tc, ts, ps_out, ph_src, pk2, pk, ph_tgt, pk32, send1, xa, xb, send2, recv2,
     ps_send, ps_recv, pt_send, pt_recv, c1_send, c1_recv, c2_send, c2_recv,
 ):
     s_me = lax.axis_index("src")
@@ -119,8 +132,8 @@
         pltpu.make_async_copy(a, b, in_sem.at[i])
         for i, (a, b) in enumerate(
             (
-                (sphase_h, sphase), (lphase_h.at[0:near], lphase.at[0:near]), (leaf_h, leaf),
-                (lint_h.at[0:LOCAL_SRC], lint.at[0:LOCAL_SRC]), (values_h, values),
+                (sphase_h, sphase), (leaf_h, leaf), (values_h, values),
+                (lphase_h.at[0:near], lphase.at[0:near]), (lint_h.at[0:LOCAL_SRC], lint.at[0:LOCAL_SRC]),
                 (lphase_h.at[near:N], lphase.at[near:N]), (mphase_h, mphase),
                 (lint_h.at[LOCAL_SRC:N], lint.at[LOCAL_SRC:N]),
                 (fphase_h, fphase), (tphase_h, tphase), (mint_h, mint), (fint_h, fint),
@@ -130,17 +143,31 @@
     for load in loads:
         load.start()
 
-    sgn = jnp.where(lane_low((R, wd), half), -1.0, 1.0)
+    low = lane_low((R, wd), half)
 
     def put(idx, angle):
-        c, s = cos_sin(angle * sgn)
+        c, s = cos_sin(angle)
         tc[idx] = c
-        ts[idx] = s
-
-    def put_level(n, prev, own, other, h):
-        oth = xor_rows(other, h)
-        put(2 * n, own if prev is None else prev + own)
-        put(2 * n + 1, oth if prev is None else prev + oth)
+        ts[idx] = jnp.where(low, -s, s)
+
+    def put_two(ia, ib, packed):
+        c, s = cos_sin(packed)
+        cr = pltpu.roll(c, half, 1)
+        sr = pltpu.roll(s, half, 1)
+        tc[ia] = jnp.where(low, c, cr)
+        tc[ib] = jnp.where(low, cr, c)
+        ts[ia] = jnp.where(low, -s, sr)
+        ts[ib] = jnp.where(low, -sr, s)
+
+    def put_level(n, prev, pair, h):
+        packed = jnp.where(low, pair, xor_rows(pair, h))
+        put_two(2 * n, 2 * n + 1, packed if prev is None else prev + packed)
+
+    def both(a, b):
+        return jnp.concatenate([a, b], -1)
+
+    def lpair(n):
+        return both(lphase[n, 0], lphase[n, 1])
 
     def lp(n, q):
         return dup(lphase[n, q])
@@ -167,7 +194,7 @@
     def ps_copy(j):
         e = xor_index(s_me, j, S)
         return pltpu.make_async_remote_copy(
-            src_ref=ps_out.at[:, blk(e), :], dst_ref=ph_src.at[:, blk(s_me), :],
+            src_ref=ps_out.at[e], dst_ref=ph_src.at[s_me],
             send_sem=ps_send, recv_sem=ps_recv, device_id=(e, t_me), device_id_type=MESH,
         )
 
@@ -185,17 +212,17 @@
             send_sem=c1_send, recv_sem=c1_recv, device_id=(e, t_me), device_id_type=MESH,
         )
 
-    def c2_copy(i, j):
+    def c2_copy(j):
         e = xor_index(t_me, j, T)
         return pltpu.make_async_remote_copy(
-            src_ref=send2.at[i, e], dst_ref=recv2.at[i, t_me],
-            send_sem=c2_send, recv_sem=c2_recv.at[i], device_id=(s_me, e), device_id_type=MESH,
+            src_ref=send2.at[e], dst_ref=recv2.at[t_me],
+            send_sem=c2_send, recv_sem=c2_recv, device_id=(s_me, e), device_id_type=MESH,
         )
 
     s_one = (xor_index(s_me, 1, S), t_me)
     t_one = (s_me, xor_index(t_me, 1, T))
     ps_all = pltpu.make_async_remote_copy(
-        src_ref=ps_out.at[:, pl.ds(0, R - T), :], dst_ref=ph_src.at[:, pl.ds(0, R - T), :],
+        src_ref=ps_out.at[pl.ds(0, S - 1)], dst_ref=ph_src.at[pl.ds(0, S - 1)],
         send_sem=ps_send, recv_sem=ps_recv, device_id=s_one, device_id_type=MESH,
     )
     pt_all = pltpu.make_async_remote_copy(
@@ -207,14 +234,16 @@
         send_sem=c1_send, recv_sem=c1_recv, device_id=s_one, device_id_type=MESH,
     )
 
-    def c2_all(i, n):
-        return pltpu.make_async_remote_copy(
-            src_ref=send2.at[pl.ds(i, n), pl.ds(0, T - 1)], dst_ref=recv2.at[pl.ds(i, n), pl.ds(0, T - 1)],
-            send_sem=c2_send, recv_sem=c2_recv.at[i], device_id=t_one, device_id_type=MESH,
-        )
+    c2_all = pltpu.make_async_remote_copy(
+        src_ref=send2.at[pl.ds(0, T - 1)], dst_ref=recv2.at[pl.ds(0, T - 1)],
+        send_sem=c2_send, recv_sem=c2_recv, device_id=t_one, device_id_type=MESH,
+    )
+
+    def spread(table, idx, i):
+        return jnp.stack([table[idx, pl.ds(i * T + t, 8, stride=0), :] for t in range(T)], 0)
 
     def tab(idx, i):
-        return tc[idx, blk(i), :][:, None, :], ts[idx, blk(i), :][:, None, :]
+        return spread(tc, idx, i), spread(ts, idx, i)
 
     def split(y):
         y = y.reshape(T, rhs, 2 * wd)
@@ -222,7 +251,7 @@
 
     def rot(v, sw, idx, i):
         c, s = tab(idx, i)
-        return v * c + sw * s
+        return jnp.concatenate([v[:, r : r + 8] * c + sw[:, r : r + 8] * s for r in range(0, rhs, 8)], 1)
 
     def dot(x, m):
         return jnp.dot(x, m, preferred_element_type=F32)
@@ -239,75 +268,71 @@
         x = jnp.concatenate([own, oth], -1).reshape(rows, 2 * wd)
         return dot(x, w[n, :, :wd]).reshape(T, rhs, wd)
 
-    for load in loads[:4]:
+    for load in loads[:3]:
         load.wait()
 
     c, s = cos_sin(point_rows(sphase))
     tc[I_SRC] = jnp.where(lane_low(c.shape, half), c, -s)
+    fill(wl, 0, leaf[...])
+    blocks = [xor_index(s_me, j, S) for j in range(S)]
+
+    def leaf_part(e):
+        at = pl.multiple_of(e * span, span)
+        parts = []
+        for p in range(T // 2):
+            parts.extend(dup_halves(values[:, pl.ds(pl.multiple_of(at + p * wd, wd), wd)], half))
+        c = spread(tc, I_SRC, e)
+        x = jnp.stack(parts, 0)
+        x = jnp.concatenate([x[:, r : r + 8] * c for r in range(0, rhs, 8)], 1)
+        return x.astype(BF16).reshape(rows, wd)
+
+    for j, e in enumerate(blocks):
+        xb[j, :, :wd] = leaf_part(e)
+
+    for load in loads[3:7]:
+        load.wait()
+
     for n in range(LOCAL_SRC):
-        put_level(n, None if n == 0 else lp(n - 1, 2), lp(n, 0), lp(n, 1), 2**n)
-    put(I_SEND1, lp(LOCAL_SRC - 1, 2) + lp(LOCAL_SRC, 0))
-    fill(wl, 0, leaf[...])
-    for n in range(LOCAL_SRC):
+        put_level(n, None if n == 0 else lp(n - 1, 2), lpair(n), 2**n)
         fill(w.at[n], 0, lint[n, 0])
         fill(w.at[n], 2 * half, lint[n, 1])
-
-    def src_part(js):
-        blocks = [xor_index(s_me, j, S) for j in js]
-        state = []
-        for e in blocks:
-            at = pl.multiple_of(e * span, span)
-            parts = []
-            for p in range(T // 2):
-                parts.extend(dup_halves(values[:, pl.ds(pl.multiple_of(at + p * wd, wd), wd)], half))
-            x = jnp.stack(parts, 0) * tc[I_SRC, blk(e), :][:, None, :]
-            state.append(split(dot(x.astype(BF16).reshape(rows, wd), wl[...])))
+    put(I_SEND1, lp(LOCAL_SRC - 1, 2) + lp(LOCAL_SRC, 0))
+
+    src_pairs = [(lphase.at[n, 0], lphase.at[n, 1]) for n in range(LOCAL_SRC, K)]
+    src_pairs += pairs_of([lphase.at[n, 2] for n in range(LOCAL_SRC, K)])
+    tgt_pairs = [(mphase.at[0], mphase.at[1])]
+    tgt_pairs += [(lphase.at[n, 0], lphase.at[n, 1]) for n in range(K, M)]
+    tgt_pairs += pairs_of([lphase.at[n, 2] for n in range(K, M - 1)])
+    Q = len(tgt_pairs)
+
+    def pack():
+        for q, (a, b) in enumerate(src_pairs):
+            code = encode(both(a[...], b[...]))
+            for e in range(S):
+                ps_out[e, q * T : (q + 1) * T, :] = code[e * T : (e + 1) * T].astype(SENT)
+        for q, (a, b) in enumerate(tgt_pairs):
+            pk2[q * R : (q + 1) * R, :] = both(a[...], b[...])
+        for d in range(T):
+            pk[d] = encode(pk2[pl.ds(d, Q * S, stride=T), :]).astype(SENT)
+
+    pack()
+    for js in groups_of(S, SRC_GROUPS):
+        state = [split(dot(xb[j, :, :wd], wl[...])) for j in js]
         for n in range(LOCAL_SRC):
-            state = [step(v, sw, n, e, 2**n) for e, (v, sw) in zip(blocks, state)]
-        for j, e, (v, sw) in zip(js, blocks, state):
-            y = rot(v, sw, I_SEND1, e).astype(BF16).reshape(rows, wd)
+            state = [step(v, sw, n, blocks[j], 2**n) for j, (v, sw) in zip(js, state)]
+        for j, (v, sw) in zip(js, state):
+            y = rot(v, sw, I_SEND1, blocks[j]).astype(BF16).reshape(rows, wd)
             if j:
                 send1[j] = y
             else:
                 xa[s_me, :, :wd] = y
-
-    def c1_start(js):
-        for j in js:
-            if j:
-                c1_copy(j).start()
-
-    for load in loads[4:7]:
-        load.wait()
-
-    def pick(arrays, q):
-        a = arrays[2 * q]()
-        b = arrays[2 * q + 1]() if 2 * q + 1 < len(arrays) else a
-        return jnp.concatenate([a, b], -1)
-
-    src_arrays = [functools.partial(lambda n, q: lphase[n, q], n, q) for n in range(LOCAL_SRC, K) for q in range(3)]
-    for q in range(ps_out.shape[0]):
-        ps_out[q] = pick(src_arrays, q)
-
-    tgt_arrays = [functools.partial(lambda q: mphase[q], q) for q in range(2)]
-    tgt_arrays += [functools.partial(lambda n, q: lphase[n, q], n, q) for n in range(K, M) for q in range(3)]
-    tgt_arrays = tgt_arrays[:-1]
-    Q = (len(tgt_arrays) + 1) // 2
-    for q in range(Q):
-        pk2[q * R : (q + 1) * R, :] = pick(tgt_arrays, q)
-    for d in range(T):
-        pk[d, 0 : Q * S, :] = pk2[pl.ds(d, Q * S, stride=T), :]
-
-    order = [tuple(S - 1 - i for i in g) for g in groups_of(S, SRC_GROUPS)]
-    src_part(order[0])
     pl.semaphore_wait(barrier, S - 1 + T - 1)
     for j in range(S - 1, 0, -1):
         ps_copy(j).start()
-    c1_start(order[0])
     for j in range(T - 1, 0, -1):
         pt_copy(j).start()
-    for js in order[1:]:
-        src_part(js)
-        c1_start(js)
+    for j in range(S - 1, 0, -1):
+        c1_copy(j).start()
 
     for load in loads[7:]:
         load.wait()
@@ -317,41 +342,29 @@
     fill(wm, 0, mint[...])
     fill(wf, 0, fint[...])
 
-    ph_src[:, blk(s_me), :] = ps_out[:, blk(s_me), :]
+    ph_src[s_me] = ps_out[s_me]
     ph_tgt[t_me] = pk[t_me]
 
     for n in range(M, N):
-        put_level(n, lp(n - 1, 2), lp(n, 0), lp(n, 1), 2 ** (n - M))
-    put(I_FIN, lp(N - 1, 2) + dup(fphase[...]))
-    put(I_TGT, point_rows(tphase))
+        put_level(n, lp(n - 1, 2), lpair(n), 2 ** (n - M))
+    put_two(I_FIN, I_TGT, jnp.where(low, lp(N - 1, 2) + dup(fphase[...]), point_rows(tphase)))
 
     ps_all.wait_recv()
-    sang = []
-    for q in range(ps_out.shape[0]):
-        sang.extend(dup_halves(ph_src[q], half))
-    for b in range(src_bits):
-        n = LOCAL_SRC + b
-        if b == 0:
-            put(2 * n + 1, xor_rows(sang[1], T) - sang[0])
-        else:
-            put_level(n, sang[3 * b - 1], sang[3 * b], sang[3 * b + 1], T * 2**b)
-
     pt_all.wait_recv()
-    ang = []
-    for q in range(Q):
-        packed = jnp.concatenate([ph_tgt[:, q * S + i, :] for i in range(S)], 0)
-        ang.extend(dup_halves(packed, half))
-    put(I_MID, sang[3 * src_bits - 1] + ang[0])
-    for b in range(tgt_bits):
-        n = K + b
-        put_level(n, ang[1] if b == 0 else ang[3 * b + 1], ang[3 * b + 2], ang[3 * b + 3], 2**b)
-
     c1_all.wait_recv()
-
+    got = [decode(ph_src[i].astype(F32)) for i in range(S)]
+    sang = [jnp.concatenate([x[q * T : (q + 1) * T] for x in got], 0) for q in range(len(src_pairs))]
+    sres = []
+    for q in range(src_bits, len(src_pairs)):
+        sres.extend(dup_halves(sang[q], half))
+    own, oth = dup_halves(sang[0], half)
+    put(2 * LOCAL_SRC + 1, xor_rows(oth, T) - own)
     bufs = (xa, xb)
     for b in range(src_bits):
         n = LOCAL_SRC + b
         dst = bufs[b % 2]
+        if b:
+            put_level(n, sres[b - 1], sang[b], T * 2**b)
         for i in range(S):
             if b == 0:
                 v = xa[i, :, :wd].astype(F32).reshape(T, rhs, wd)
@@ -360,6 +373,17 @@
                 v, sw = split(dot(bufs[(b - 1) % 2][i], w[n - 1]))
                 dst[i, :, :wd] = rot(v, sw, 2 * n, i).astype(BF16).reshape(rows, wd)
             dst[i ^ 2**b, :, wd:] = rot(v, sw, 2 * n + 1, i).astype(BF16).reshape(rows, wd)
+
+    for d in range(T):
+        pk32[d] = decode(ph_tgt[d].astype(F32))
+    tang = [jnp.concatenate([pk32[:, q * S + i, :] for i in range(S)], 0) for q in range(Q)]
+    mid0, mid1 = dup_halves(tang[0], half)
+    tres = [mid1]
+    for q in range(1 + tgt_bits, Q):
+        tres.extend(dup_halves(tang[q], half))
+    put(I_MID, sres[src_bits - 1] + mid0)
+    for b in range(tgt_bits):
+        put_level(K + b, tres[b], tang[1 + b], 2**b)
 
     for blocks in groups_of(S, MID_GROUPS):
         state = [split(dot(bufs[(src_bits - 1) % 2][i], w[K - 1])) for i in blocks]
@@ -371,20 +395,18 @@
             else:
                 state = [last_step(v, sw, K + b, i, 2**b) for i, (v, sw) in zip(blocks, state)]
         for i, v in zip(blocks, state):
-            send2[i] = v.astype(BF16)
-        for i in blocks:
-            for j in range(T - 1, 0, -1):
-                c2_copy(i, j).start()
-            recv2[i, t_me] = send2[i, t_me]
+            send2[:, i] = v.astype(BF16)
+    for j in range(T - 1, 0, -1):
+        c2_copy(j).start()
+    recv2[t_me] = send2[t_me]
 
     low3 = lane_low((rhs, wd), half)
 
+    c2_all.wait_recv()
     for blocks in groups_of(S, FIN_GROUPS):
-        for i in blocks:
-            c2_all(i, 1).wait_recv()
         state = []
         for i in blocks:
-            v = recv2[i].astype(F32)
+            v = recv2[:, i].astype(F32)
             state.append((v, pltpu.roll(v, half, 2)))
         for n in range(M, N):
             state = [step(v, sw, n, i, 2 ** (n - M)) for i, (v, sw) in zip(blocks, state)]
@@ -400,7 +422,7 @@
     ps_all.wait_send()
     pt_all.wait_send()
     c1_all.wait_send()
-    c2_all(0, S).wait_send()
+    c2_all.wait_send()
 
 
 def shards(
@@ -418,8 +440,8 @@
     src_bits = S.bit_length() - 1
     tgt_bits = T.bit_length() - 1
     assert N == LOCAL_SRC + src_bits + tgt_bits + LOCAL_TGT
-    Q1 = (3 * src_bits + 1) // 2
-    Q = (1 + 3 * tgt_bits + 1) // 2
+    Q1 = src_bits + (src_bits + 1) // 2
+    Q = 1 + tgt_bits + tgt_bits // 2
     ntab = 2 * N + 5
     vm = pltpu.VMEM
     dma = pltpu.SemaphoreType.DMA
@@ -437,13 +459,13 @@
             vm((N, 2 * wd, 2 * wd), BF16), vm((wd, 2 * wd), BF16),
             vm((wd, 2 * wd), BF16), vm((wd, 2 * wd), BF16),
             vm((ntab, R, wd), F32), vm((ntab, R, wd), F32),
-            vm((Q1, R, wd), F32), vm((Q1, R, wd), F32), vm((Q * R, wd), F32),
-            vm((T, Q * S, wd), F32), vm((T, Q * S, wd), F32),
+            vm((S, Q1 * T, wd), SENT), vm((S, Q1 * T, wd), SENT), vm((Q * R, wd), F32),
+            vm((T, Q * S, wd), SENT), vm((T, Q * S, wd), SENT), vm((T, Q * S, wd), F32),
             vm((S, T * rhs, wd), BF16),
             vm((S, T * rhs, 2 * wd), BF16), vm((S, T * rhs, 2 * wd), BF16),
-            vm((S, T, rhs, wd), BF16), vm((S, T, rhs, wd), BF16),
+            vm((T, S, rhs, wd), BF16), vm((T, S, rhs, wd), BF16),
             dma(()), dma(()), dma(()), dma(()),
-            dma(()), dma(()), dma(()), dma((S,)),
+            dma(()), dma(()), dma(()), dma(()),
         ],
         compiler_params=pltpu.CompilerParams(
             collective_id=0, has_side_effects=True, vmem_limit_bytes=VLIM

time: 17.4 us -> 16.7 us (0.960)
  Pallas kernels: 16.5 us -> 15.8 us
    pallas_call x1, Pallas kernels: 16.5 us -> 15.8 us  [shards(): pl.pallas_call(functools.partial(kernel, S, T, N, src_bits, tgt_bits), ou...]
where the time goes in v2:
time: 16.7 us; the launch traced here: 16.5 us
  Pallas kernels  15.8 us (95%)
  local copies, waits for them, and re-layouts  0.71 us (4%)
    pallas_call x1, Pallas kernels, shards(): pl.pallas_call(functools.partial(kernel, S, T, N, src_bits, tgt_bits), ou...  15.8 us
    unnamed x1, local copies, waits for them, and re-layouts  0.71 us

profile of v2, /device:TPU:0, one launch (start us, length us, event | category | flops | bytes accessed | tf_op | source)
XLA Modules:
  0.0 16.5 jit_solution(12103097239748446073)
XLA Ops:
  0.0 15.8 %shard_map.100 = f32[2,16,2048]{2,1,0:T(8,128)S(1)} custom-call(f32[16,2048]{1,0:T(8,128)} %values_h.1, f32[16,128]{1,0:T(8,128)} %bitcast.2, bf16[64,64]{1,0:T(8,128)(2,1)} %leaf_h.1, bf16[11,2,64,64]{3,2,1,0:T(8,128)(2,1)} %lint_h.1, f32[11,3,32,64]{3,2,1,0:T(8,128)} %lphase_h.1, bf16[64,64]{1,0:T(8,128)(2,1)} %mint_h.1, f32[2,32,64]{2,1,0:T(8,128)} %mphase_h.1, ...), custom_call_target="tpu_custom_call" | custom-call | tf_op jit(solution)/shard_map/pallas_call | solution.py:452
  15.8 0.7 %copy.12 = f32[2,16,2048]{2,1,0:T(8,128)} copy(f32[2,16,2048]{2,1,0:T(8,128)S(1)} %shard_map.100) | data formatting | bytes 524288

commit v3 on v2

--- a/solution.py
+++ b/solution.py
@@ -10,13 +10,15 @@
 LOCAL_SRC = 3
 LOCAL_TGT = 3
 MESH = pl.DeviceIdType.MESH
-SRC_GROUPS = (4,)
+FIRST = 8
+AHEAD = 2
 MID_GROUPS = (4,)
 FIN_GROUPS = (4,)
 VLIM = 40 * 1024 * 1024
 F32 = jnp.float32
 BF16 = jnp.bfloat16
-SENT = jnp.float32
+SENT = jnp.bfloat16
+SEG = 64
 
 PI_HI = 3.140625
 PI_LO = 9.67653589793e-4
@@ -78,11 +80,17 @@
 
 
 def encode(x):
-    return x
-
-
-def decode(x):
-    return x
+    a = jnp.abs(x) * (SEG / 3.141592653589793)
+    k = jnp.floor(a)
+    v = (1.0 + (a - k)) * jnp.exp2(k - SEG / 2)
+    return jnp.where(x < 0, -v, v)
+
+
+def decode(y):
+    u = jnp.abs(y)
+    k = jnp.floor(jnp.log2(u))
+    r = (k + u * jnp.exp2(-k) + (SEG / 2 - 1)) * (3.141592653589793 / SEG)
+    return jnp.where(y < 0, -r, r)
 
 
 def groups_of(n, sizes):
@@ -105,13 +113,13 @@
     S, T, levels, src_bits, tgt_bits,
     values_h, sphase_h, leaf_h, lint_h, lphase_h, mint_h, mphase_h, fphase_h, fint_h, tphase_h,
     out,
-    values, sphase, leaf, lint, lphase, mint, mphase, fphase, fint, tphase, in_sem,
+    values, lint, lphase, points, mats, phases, in_sem,
     w, wl, wm, wf, tc, ts, ps_out, ph_src, pk2, pk, ph_tgt, pk32, send1, xa, xb, send2, recv2,
     ps_send, ps_recv, pt_send, pt_recv, c1_send, c1_recv, c2_send, c2_recv,
 ):
     s_me = lax.axis_index("src")
     t_me = lax.axis_index("tgt")
-    half = leaf.shape[1]
+    half = mats.shape[1]
     wd = 2 * half
     span = T * half
     R = S * T
@@ -127,50 +135,58 @@
     for j in range(1, S):
         pl.semaphore_signal(barrier, inc=1, device_id=(lax.rem(s_me + j, S), t_me), device_id_type=MESH)
 
-    near = LOCAL_SRC + 1
     loads = [
         pltpu.make_async_copy(a, b, in_sem.at[i])
-        for i, (a, b) in enumerate(
-            (
-                (sphase_h, sphase), (leaf_h, leaf), (values_h, values),
-                (lphase_h.at[0:near], lphase.at[0:near]), (lint_h.at[0:LOCAL_SRC], lint.at[0:LOCAL_SRC]),
-                (lphase_h.at[near:N], lphase.at[near:N]), (mphase_h, mphase),
-                (lint_h.at[LOCAL_SRC:N], lint.at[LOCAL_SRC:N]),
-                (fphase_h, fphase), (tphase_h, tphase), (mint_h, mint), (fint_h, fint),
-            )
+        for a, b, i in (
+            (sphase_h, points.at[0], 0), (tphase_h, points.at[1], 0),
+            (leaf_h, mats.at[0], 1), (mint_h, mats.at[1], 1), (fint_h, mats.at[2], 1),
+            (values_h.at[:, 0:span], values.at[:, 0:span], 2),
+            (lphase_h.at[0:K, :, 0:T], lphase.at[0:K, :, 0:T], 3),
+            (lint_h.at[0:LOCAL_SRC], lint.at[0:LOCAL_SRC], 4),
+            (values_h.at[:, span : S * span], values.at[:, span : S * span], 5),
+            (lphase_h.at[0:K, :, T:R], lphase.at[0:K, :, T:R], 6),
+            (lphase_h.at[K:N], lphase.at[K:N], 7),
+            (mphase_h, phases.at[0:2], 8), (fphase_h, phases.at[2], 8),
+            (lint_h.at[LOCAL_SRC:N], lint.at[LOCAL_SRC:N], 9),
         )
     ]
-    for load in loads:
+    both_points = pltpu.make_async_copy(points, points, in_sem.at[0])
+    all_mats = pltpu.make_async_copy(mats, mats, in_sem.at[1])
+    all_phases = pltpu.make_async_copy(phases, phases, in_sem.at[8])
+    for load in loads[:FIRST]:
         load.start()
 
     low = lane_low((R, wd), half)
 
-    def put(idx, angle):
+    def put(idx, angle, at=0):
+        n = angle.shape[0]
         c, s = cos_sin(angle)
-        tc[idx] = c
-        ts[idx] = jnp.where(low, -s, s)
-
-    def put_two(ia, ib, packed):
+        tc[idx, at : at + n] = c
+        ts[idx, at : at + n] = jnp.where(low[:n], -s, s)
+
+    def put_two(ia, ib, packed, at=0):
+        n = packed.shape[0]
+        m = low[:n]
         c, s = cos_sin(packed)
         cr = pltpu.roll(c, half, 1)
         sr = pltpu.roll(s, half, 1)
-        tc[ia] = jnp.where(low, c, cr)
-        tc[ib] = jnp.where(low, cr, c)
-        ts[ia] = jnp.where(low, -s, sr)
-        ts[ib] = jnp.where(low, -sr, s)
-
-    def put_level(n, prev, pair, h):
-        packed = jnp.where(low, pair, xor_rows(pair, h))
-        put_two(2 * n, 2 * n + 1, packed if prev is None else prev + packed)
+        tc[ia, at : at + n] = jnp.where(m, c, cr)
+        tc[ib, at : at + n] = jnp.where(m, cr, c)
+        ts[ia, at : at + n] = jnp.where(m, -s, sr)
+        ts[ib, at : at + n] = jnp.where(m, -sr, s)
+
+    def put_level(n, prev, pair, h, at=0):
+        packed = jnp.where(low[: pair.shape[0]], pair, xor_rows(pair, h))
+        put_two(2 * n, 2 * n + 1, packed if prev is None else prev + packed, at)
 
     def both(a, b):
         return jnp.concatenate([a, b], -1)
 
-    def lpair(n):
-        return both(lphase[n, 0], lphase[n, 1])
-
-    def lp(n, q):
-        return dup(lphase[n, q])
+    def lpair(n, a=0, b=R):
+        return both(lphase[n, 0, a:b], lphase[n, 1, a:b])
+
+    def lp(n, q, a=0, b=R):
+        return dup(lphase[n, q, a:b])
 
     I_SEND1, I_MID, I_FIN, I_TGT, I_SRC = (2 * N + i for i in range(5))
 
@@ -191,8 +207,7 @@
     def blk(i):
         return pl.ds(pl.multiple_of(i * T, T), T)
 
-    def ps_copy(j):
-        e = xor_index(s_me, j, S)
+    def ps_copy(e):
         return pltpu.make_async_remote_copy(
             src_ref=ps_out.at[e], dst_ref=ph_src.at[s_me],
             send_sem=ps_send, recv_sem=ps_recv, device_id=(e, t_me), device_id_type=MESH,
@@ -205,19 +220,22 @@
             send_sem=pt_send, recv_sem=pt_recv, device_id=(s_me, e), device_id_type=MESH,
         )
 
-    def c1_copy(j):
-        e = xor_index(s_me, j, S)
+    def c1_copy(e):
         return pltpu.make_async_remote_copy(
-            src_ref=send1.at[j], dst_ref=xa.at[s_me, :, pl.ds(0, wd)],
+            src_ref=send1.at[e], dst_ref=xa.at[s_me, :, pl.ds(0, wd)],
             send_sem=c1_send, recv_sem=c1_recv, device_id=(e, t_me), device_id_type=MESH,
         )
 
-    def c2_copy(j):
-        e = xor_index(t_me, j, T)
+    def c2_copy(k):
+        e = k + (t_me <= k).astype(jnp.int32)
         return pltpu.make_async_remote_copy(
             src_ref=send2.at[e], dst_ref=recv2.at[t_me],
             send_sem=c2_send, recv_sem=c2_recv, device_id=(s_me, e), device_id_type=MESH,
         )
+
+    def pt_start():
+        for j in range(T - 1, 0, -1):
+            pt_copy(j).start()
 
     s_one = (xor_index(s_me, 1, S), t_me)
     t_one = (s_me, xor_index(t_me, 1, T))
@@ -268,90 +286,151 @@
         x = jnp.concatenate([own, oth], -1).reshape(rows, 2 * wd)
         return dot(x, w[n, :, :wd]).reshape(T, rhs, wd)
 
-    for load in loads[:3]:
-        load.wait()
-
-    c, s = cos_sin(point_rows(sphase))
+    both_points.wait()
+    all_mats.wait()
+    loads[5].wait()
+    for load in loads[FIRST:]:
+        load.start()
+    c, s = cos_sin(point_rows(points.at[0]))
     tc[I_SRC] = jnp.where(lane_low(c.shape, half), c, -s)
-    fill(wl, 0, leaf[...])
-    blocks = [xor_index(s_me, j, S) for j in range(S)]
-
+    fill(wl, 0, mats[0])
     def leaf_part(e):
-        at = pl.multiple_of(e * span, span)
         parts = []
         for p in range(T // 2):
-            parts.extend(dup_halves(values[:, pl.ds(pl.multiple_of(at + p * wd, wd), wd)], half))
+            parts.extend(dup_halves(values[:, e * span + p * wd : e * span + (p + 1) * wd], half))
         c = spread(tc, I_SRC, e)
         x = jnp.stack(parts, 0)
         x = jnp.concatenate([x[:, r : r + 8] * c for r in range(0, rhs, 8)], 1)
         return x.astype(BF16).reshape(rows, wd)
 
-    for j, e in enumerate(blocks):
-        xb[j, :, :wd] = leaf_part(e)
-
-    for load in loads[3:7]:
-        load.wait()
-
-    for n in range(LOCAL_SRC):
-        put_level(n, None if n == 0 else lp(n - 1, 2), lpair(n), 2**n)
-        fill(w.at[n], 0, lint[n, 0])
-        fill(w.at[n], 2 * half, lint[n, 1])
-    put(I_SEND1, lp(LOCAL_SRC - 1, 2) + lp(LOCAL_SRC, 0))
+    xb[0, :, :wd] = leaf_part(0)
+
+    loads[6].wait()
+    loads[7].wait()
 
     src_pairs = [(lphase.at[n, 0], lphase.at[n, 1]) for n in range(LOCAL_SRC, K)]
     src_pairs += pairs_of([lphase.at[n, 2] for n in range(LOCAL_SRC, K)])
-    tgt_pairs = [(mphase.at[0], mphase.at[1])]
+    tgt_pairs = [(phases.at[0], phases.at[1])]
     tgt_pairs += [(lphase.at[n, 0], lphase.at[n, 1]) for n in range(K, M)]
     tgt_pairs += pairs_of([lphase.at[n, 2] for n in range(K, M - 1)])
     Q = len(tgt_pairs)
 
-    def pack():
+    def src_part(blocks):
+        a, b = blocks[0] * T, blocks[-1] * T + T
+        state = [split(dot(xb[e, :, :wd], wl[...])) for e in blocks]
+        for n in range(LOCAL_SRC):
+            put_level(n, None if n == 0 else lp(n - 1, 2, a, b), lpair(n, a, b), 2**n, a)
+            if blocks[0] == 0:
+                fill(w.at[n], 0, lint[n, 0])
+                fill(w.at[n], 2 * half, lint[n, 1])
+            state = [step(v, sw, n, e, 2**n) for e, (v, sw) in zip(blocks, state)]
+        put(I_SEND1, lp(LOCAL_SRC - 1, 2, a, b) + lp(LOCAL_SRC, 0, a, b), a)
+        for e, (v, sw) in zip(blocks, state):
+            send1[e] = rot(v, sw, I_SEND1, e).astype(BF16).reshape(rows, wd)
+
+    def pack_src(blocks):
         for q, (a, b) in enumerate(src_pairs):
-            code = encode(both(a[...], b[...]))
-            for e in range(S):
-                ps_out[e, q * T : (q + 1) * T, :] = code[e * T : (e + 1) * T].astype(SENT)
+            for e in blocks:
+                at = slice(e * T, (e + 1) * T)
+                ps_out[e, q * T : (q + 1) * T, :] = encode(both(a[at], b[at])).astype(SENT)
+
+    def pack_tgt():
         for q, (a, b) in enumerate(tgt_pairs):
             pk2[q * R : (q + 1) * R, :] = both(a[...], b[...])
         for d in range(T):
             pk[d] = encode(pk2[pl.ds(d, Q * S, stride=T), :]).astype(SENT)
 
-    pack()
-    for js in groups_of(S, SRC_GROUPS):
-        state = [split(dot(xb[j, :, :wd], wl[...])) for j in js]
-        for n in range(LOCAL_SRC):
-            state = [step(v, sw, n, blocks[j], 2**n) for j, (v, sw) in zip(js, state)]
-        for j, (v, sw) in zip(js, state):
-            y = rot(v, sw, I_SEND1, blocks[j]).astype(BF16).reshape(rows, wd)
-            if j:
-                send1[j] = y
-            else:
-                xa[s_me, :, :wd] = y
+    pack_src([0])
+
+    def wait_rest():
+        loads[8].wait()
+        loads[9].wait()
+
+    def pack_rest():
+        loads[10].wait()
+        all_phases.wait()
+        pack_tgt()
+
+    @pl.when(s_me == 0)
+    def _():
+        wait_rest()
+        pack_rest()
+
+    rest = list(range(1, S))
+
+    def src_rest():
+        for e in rest:
+            xb[e, :, :wd] = leaf_part(e)
+        pack_src(rest)
+        src_part(rest)
+
+    late = t_me >= T // 2
+
+    @pl.when(jnp.logical_not(late))
+    def _():
+        src_part([0])
+
+        @pl.when(s_me != 0)
+        def _():
+            wait_rest()
+
+        src_rest()
+
     pl.semaphore_wait(barrier, S - 1 + T - 1)
-    for j in range(S - 1, 0, -1):
-        ps_copy(j).start()
-    for j in range(T - 1, 0, -1):
-        pt_copy(j).start()
-    for j in range(S - 1, 0, -1):
-        c1_copy(j).start()
-
-    for load in loads[7:]:
-        load.wait()
-    for n in range(LOCAL_SRC, N):
+
+    @pl.when(s_me != 0)
+    def _():
+        ps_copy(0).start()
+
+    @pl.when(s_me == 0)
+    def _():
+        pt_start()
+
+    @pl.when(late)
+    def _():
+        src_part([0])
+
+    @pl.when(s_me != 0)
+    def _():
+        c1_copy(0).start()
+
+        @pl.when(late)
+        def _():
+            wait_rest()
+
+        pack_rest()
+        pt_start()
+
+    @pl.when(late)
+    def _():
+        src_rest()
+
+    def others_start():
+        for e in rest:
+            @pl.when(s_me != e)
+            def _():
+                ps_copy(e).start()
+                c1_copy(e).start()
+
+    @pl.when(s_me != 0)
+    def _():
+        others_start()
+
+    xa[s_me, :, :wd] = send1[s_me]
+
+    loads[13].wait()
+    for n in range(LOCAL_SRC, M):
         fill(w.at[n], 0, lint[n, 0])
         fill(w.at[n], 2 * half, lint[n, 1])
-    fill(wm, 0, mint[...])
-    fill(wf, 0, fint[...])
-
+    fill(wm, 0, mats[1])
     ph_src[s_me] = ps_out[s_me]
     ph_tgt[t_me] = pk[t_me]
 
-    for n in range(M, N):
-        put_level(n, lp(n - 1, 2), lpair(n), 2 ** (n - M))
-    put_two(I_FIN, I_TGT, jnp.where(low, lp(N - 1, 2) + dup(fphase[...]), point_rows(tphase)))
+    @pl.when(s_me == 0)
+    def _():
+        others_start()
 
     ps_all.wait_recv()
-    pt_all.wait_recv()
-    c1_all.wait_recv()
     got = [decode(ph_src[i].astype(F32)) for i in range(S)]
     sang = [jnp.concatenate([x[q * T : (q + 1) * T] for x in got], 0) for q in range(len(src_pairs))]
     sres = []
@@ -359,21 +438,9 @@
         sres.extend(dup_halves(sang[q], half))
     own, oth = dup_halves(sang[0], half)
     put(2 * LOCAL_SRC + 1, xor_rows(oth, T) - own)
-    bufs = (xa, xb)
-    for b in range(src_bits):
-        n = LOCAL_SRC + b
-        dst = bufs[b % 2]
-        if b:
-            put_level(n, sres[b - 1], sang[b], T * 2**b)
-        for i in range(S):
-            if b == 0:
-                v = xa[i, :, :wd].astype(F32).reshape(T, rhs, wd)
-                sw = pltpu.roll(v, half, 2)
-            else:
-                v, sw = split(dot(bufs[(b - 1) % 2][i], w[n - 1]))
-                dst[i, :, :wd] = rot(v, sw, 2 * n, i).astype(BF16).reshape(rows, wd)
-            dst[i ^ 2**b, :, wd:] = rot(v, sw, 2 * n + 1, i).astype(BF16).reshape(rows, wd)
-
+    for b in range(1, src_bits):
+        put_level(LOCAL_SRC + b, sres[b - 1], sang[b], T * 2**b)
+    pt_all.wait_recv()
     for d in range(T):
         pk32[d] = decode(ph_tgt[d].astype(F32))
     tang = [jnp.concatenate([pk32[:, q * S + i, :] for i in range(S)], 0) for q in range(Q)]
@@ -384,6 +451,19 @@
     put(I_MID, sres[src_bits - 1] + mid0)
     for b in range(tgt_bits):
         put_level(K + b, tres[b], tang[1 + b], 2**b)
+    c1_all.wait_recv()
+    bufs = (xa, xb)
+    for b in range(src_bits):
+        n = LOCAL_SRC + b
+        dst = bufs[b % 2]
+        for i in range(S):
+            if b == 0:
+                v = xa[i, :, :wd].astype(F32).reshape(T, rhs, wd)
+                sw = pltpu.roll(v, half, 2)
+            else:
+                v, sw = split(dot(bufs[(b - 1) % 2][i], w[n - 1]))
+                dst[i, :, :wd] = rot(v, sw, 2 * n, i).astype(BF16).reshape(rows, wd)
+            dst[i ^ 2**b, :, wd:] = rot(v, sw, 2 * n + 1, i).astype(BF16).reshape(rows, wd)
 
     for blocks in groups_of(S, MID_GROUPS):
         state = [split(dot(bufs[(src_bits - 1) % 2][i], w[K - 1])) for i in blocks]
@@ -396,8 +476,17 @@
                 state = [last_step(v, sw, K + b, i, 2**b) for i, (v, sw) in zip(blocks, state)]
         for i, v in zip(blocks, state):
             send2[:, i] = v.astype(BF16)
-    for j in range(T - 1, 0, -1):
-        c2_copy(j).start()
+    for k in range(AHEAD):
+        c2_copy(k).start()
+    for n in range(M, N):
+        fill(w.at[n], 0, lint[n, 0])
+        fill(w.at[n], 2 * half, lint[n, 1])
+    fill(wf, 0, mats[2])
+    for n in range(M, N):
+        put_level(n, lp(n - 1, 2), lpair(n), 2 ** (n - M))
+    put_two(I_FIN, I_TGT, jnp.where(low, lp(N - 1, 2) + dup(phases[2]), point_rows(points.at[1])))
+    for k in range(AHEAD, T - 1):
+        c2_copy(k).start()
     recv2[t_me] = send2[t_me]
 
     low3 = lane_low((rhs, wd), half)
@@ -454,8 +543,8 @@
         out_shape=pltpu.VMEM((2,) + source_values.shape, F32),
         in_specs=[pl.BlockSpec(memory_space=pltpu.HBM)] * 10,
         out_specs=pl.BlockSpec(memory_space=pltpu.VMEM),
-        scratch_shapes=[vm(a.shape, a.dtype) for a in args] + [
-            dma((12,)),
+        scratch_shapes=[vm(args[i].shape, args[i].dtype) for i in (0, 3, 4)] + [
+            vm((2,) + args[1].shape, F32), vm((3, half, half), BF16), vm((3, R, half), F32), dma((10,)),
             vm((N, 2 * wd, 2 * wd), BF16), vm((wd, 2 * wd), BF16),
             vm((wd, 2 * wd), BF16), vm((wd, 2 * wd), BF16),
             vm((ntab, R, wd), F32), vm((ntab, R, wd), F32),

time: 16.7 us -> 16.1 us (0.964)
  Pallas kernels: 15.8 us -> 15.2 us
    pallas_call x1, Pallas kernels: 15.8 us -> 15.2 us  [shards(): pl.pallas_call(functools.partial(kernel, S, T, N, src_bits, tgt_bits), ou...]
where the time goes in v3:
time: 16.1 us; the launch traced here: 15.9 us
  Pallas kernels  15.2 us (94%)
  local copies, waits for them, and re-layouts  0.71 us (4%)
    pallas_call x1, Pallas kernels, shards(): pl.pallas_call(functools.partial(kernel, S, T, N, src_bits, tgt_bits), ou...  15.2 us
    unnamed x1, local copies, waits for them, and re-layouts  0.71 us

profile of v3, /device:TPU:0, one launch (start us, length us, event | category | flops | bytes accessed | tf_op | source)
XLA Modules:
  0.0 15.9 jit_solution(13549910153728421276)
XLA Ops:
  0.0 15.2 %shard_map.100 = f32[2,16,2048]{2,1,0:T(8,128)S(1)} custom-call(f32[16,2048]{1,0:T(8,128)} %values_h.1, f32[16,128]{1,0:T(8,128)} %bitcast.2, bf16[64,64]{1,0:T(8,128)(2,1)} %leaf_h.1, bf16[11,2,64,64]{3,2,1,0:T(8,128)(2,1)} %lint_h.1, f32[11,3,32,64]{3,2,1,0:T(8,128)} %lphase_h.1, bf16[64,64]{1,0:T(8,128)(2,1)} %mint_h.1, f32[2,32,64]{2,1,0:T(8,128)} %mphase_h.1, ...), custom_call_target="tpu_custom_call" | custom-call | tf_op jit(solution)/shard_map/pallas_call | solution.py:541
  15.2 0.7 %copy.12 = f32[2,16,2048]{2,1,0:T(8,128)} copy(f32[2,16,2048]{2,1,0:T(8,128)S(1)} %shard_map.100) | data formatting | bytes 524288

commit v4 on v3

--- a/solution.py
+++ b/solution.py
@@ -139,10 +139,11 @@
         pltpu.make_async_copy(a, b, in_sem.at[i])
         for a, b, i in (
             (sphase_h, points.at[0], 0), (tphase_h, points.at[1], 0),
-            (leaf_h, mats.at[0], 1), (mint_h, mats.at[1], 1), (fint_h, mats.at[2], 1),
+            (lphase_h.at[0:K, :, 0:T], lphase.at[0:K, :, 0:T], 3),
             (values_h.at[:, 0:span], values.at[:, 0:span], 2),
-            (lphase_h.at[0:K, :, 0:T], lphase.at[0:K, :, 0:T], 3),
+            (leaf_h, mats.at[0], 1),
             (lint_h.at[0:LOCAL_SRC], lint.at[0:LOCAL_SRC], 4),
+            (mint_h, mats.at[1], 1), (fint_h, mats.at[2], 1),
             (values_h.at[:, span : S * span], values.at[:, span : S * span], 5),
             (lphase_h.at[0:K, :, T:R], lphase.at[0:K, :, T:R], 6),
             (lphase_h.at[K:N], lphase.at[K:N], 7),
@@ -288,7 +289,7 @@
 
     both_points.wait()
     all_mats.wait()
-    loads[5].wait()
+    loads[3].wait()
     for load in loads[FIRST:]:
         load.start()
     c, s = cos_sin(point_rows(points.at[0]))
@@ -305,8 +306,8 @@
 
     xb[0, :, :wd] = leaf_part(0)
 
-    loads[6].wait()
-    loads[7].wait()
+    loads[2].wait()
+    loads[5].wait()
 
     src_pairs = [(lphase.at[n, 0], lphase.at[n, 1]) for n in range(LOCAL_SRC, K)]
     src_pairs += pairs_of([lphase.at[n, 2] for n in range(LOCAL_SRC, K)])
@@ -364,44 +365,47 @@
         pack_src(rest)
         src_part(rest)
 
-    late = t_me >= T // 2
-
-    @pl.when(jnp.logical_not(late))
+    block_ahead = t_me < T // 2
+    all_ahead = t_me < T // 4
+
+    @pl.when(block_ahead)
     def _():
         src_part([0])
 
-        @pl.when(s_me != 0)
+    @pl.when(all_ahead & (s_me != 0))
+    def _():
+        wait_rest()
+
+    @pl.when(all_ahead)
+    def _():
+        src_rest()
+
+    pl.semaphore_wait(barrier, S - 1 + T - 1)
+
+    @pl.when(s_me != 0)
+    def _():
+        ps_copy(0).start()
+
+    @pl.when(s_me == 0)
+    def _():
+        pt_start()
+
+    @pl.when(jnp.logical_not(block_ahead))
+    def _():
+        src_part([0])
+
+    @pl.when(s_me != 0)
+    def _():
+        c1_copy(0).start()
+
+        @pl.when(jnp.logical_not(all_ahead))
         def _():
             wait_rest()
 
-        src_rest()
-
-    pl.semaphore_wait(barrier, S - 1 + T - 1)
-
-    @pl.when(s_me != 0)
-    def _():
-        ps_copy(0).start()
-
-    @pl.when(s_me == 0)
-    def _():
-        pt_start()
-
-    @pl.when(late)
-    def _():
-        src_part([0])
-
-    @pl.when(s_me != 0)
-    def _():
-        c1_copy(0).start()
-
-        @pl.when(late)
-        def _():
-            wait_rest()
-
         pack_rest()
         pt_start()
 
-    @pl.when(late)
+    @pl.when(jnp.logical_not(all_ahead))
     def _():
         src_rest()
 

time: 16.1 us -> 15.8 us (0.981)
  the two profiles are of different devices: /device:TPU:0 before, /device:TPU:1 now
where the time goes in v4:
time: 15.8 us; the launch traced here: 15.5 us
  Pallas kernels  14.8 us (94%)
  local copies, waits for them, and re-layouts  0.71 us (4%)
    pallas_call x1, Pallas kernels, shards(): pl.pallas_call(functools.partial(kernel, S, T, N, src_bits, tgt_bits), ou...  14.8 us
    unnamed x1, local copies, waits for them, and re-layouts  0.71 us

profile of v4, /device:TPU:1, one launch (start us, length us, event | category | flops | bytes accessed | tf_op | source)
XLA Modules:
  0.0 15.5 jit_solution(2395073754423467510)
XLA Ops:
  0.0 14.8 %shard_map.100 = f32[2,16,2048]{2,1,0:T(8,128)S(1)} custom-call(f32[16,2048]{1,0:T(8,128)} %values_h.1, f32[16,128]{1,0:T(8,128)} %bitcast.2, bf16[64,64]{1,0:T(8,128)(2,1)} %leaf_h.1, bf16[11,2,64,64]{3,2,1,0:T(8,128)(2,1)} %lint_h.1, f32[11,3,32,64]{3,2,1,0:T(8,128)} %lphase_h.1, bf16[64,64]{1,0:T(8,128)(2,1)} %mint_h.1, f32[2,32,64]{2,1,0:T(8,128)} %mphase_h.1, ...), custom_call_target="tpu_custom_call" | custom-call | tf_op jit(solution)/shard_map/pallas_call | solution.py:545
  14.8 0.7 %copy.12 = f32[2,16,2048]{2,1,0:T(8,128)} copy(f32[2,16,2048]{2,1,0:T(8,128)S(1)} %shard_map.100) | data formatting | bytes 524288

commit v5 on v4

--- a/solution.py
+++ b/solution.py
@@ -115,7 +115,7 @@
     out,
     values, lint, lphase, points, mats, phases, in_sem,
     w, wl, wm, wf, tc, ts, ps_out, ph_src, pk2, pk, ph_tgt, pk32, send1, xa, xb, send2, recv2,
-    ps_send, ps_recv, pt_send, pt_recv, c1_send, c1_recv, c2_send, c2_recv,
+    ps_recv, pt_recv, c1_recv, c2_recv,
 ):
     s_me = lax.axis_index("src")
     t_me = lax.axis_index("tgt")
@@ -144,16 +144,17 @@
             (leaf_h, mats.at[0], 1),
             (lint_h.at[0:LOCAL_SRC], lint.at[0:LOCAL_SRC], 4),
             (mint_h, mats.at[1], 1), (fint_h, mats.at[2], 1),
-            (values_h.at[:, span : S * span], values.at[:, span : S * span], 5),
-            (lphase_h.at[0:K, :, T:R], lphase.at[0:K, :, T:R], 6),
-            (lphase_h.at[K:N], lphase.at[K:N], 7),
-            (mphase_h, phases.at[0:2], 8), (fphase_h, phases.at[2], 8),
-            (lint_h.at[LOCAL_SRC:N], lint.at[LOCAL_SRC:N], 9),
+            (values_h.at[:, span : S * span], values.at[:, span : S * span], 0),
+            (lphase_h.at[0:K, :, T:R], lphase.at[0:K, :, T:R], 1),
+            (lphase_h.at[K:N], lphase.at[K:N], 2),
+            (mphase_h, phases.at[0:2], 5), (fphase_h, phases.at[2], 5),
+            (lint_h.at[LOCAL_SRC:N], lint.at[LOCAL_SRC:N], 6),
         )
     ]
     both_points = pltpu.make_async_copy(points, points, in_sem.at[0])
     all_mats = pltpu.make_async_copy(mats, mats, in_sem.at[1])
-    all_phases = pltpu.make_async_copy(phases, phases, in_sem.at[8])
+    all_phases = pltpu.make_async_copy(phases, phases, in_sem.at[5])
+    ps_send, c1_send, pt_send, c2_send = (in_sem.at[i] for i in (3, 4, 5, 6))
     for load in loads[:FIRST]:
         load.start()
 
@@ -488,7 +489,10 @@
     fill(wf, 0, mats[2])
     for n in range(M, N):
         put_level(n, lp(n - 1, 2), lpair(n), 2 ** (n - M))
-    put_two(I_FIN, I_TGT, jnp.where(low, lp(N - 1, 2) + dup(phases[2]), point_rows(points.at[1])))
+    put(I_FIN, lp(N - 1, 2) + dup(phases[2]))
+    c, s = cos_sin(points[1])
+    tc[I_TGT, 0 : R // 2] = c
+    ts[I_TGT, 0 : R // 2] = s
     for k in range(AHEAD, T - 1):
         c2_copy(k).start()
     recv2[t_me] = send2[t_me]
@@ -506,12 +510,15 @@
         state = [rot(v, sw, I_FIN, i).astype(BF16).reshape(rows, wd) for i, (v, sw) in zip(blocks, state)]
         state = [split(dot(x, wf[...])) for x in state]
         for i, (v, sw) in zip(blocks, state):
-            r = rot(v, sw, I_TGT, i)
-            rr = pltpu.roll(r, half, 2)
             for p in range(T // 2):
+                row = pl.ds(i * (T // 2) + p, 8, stride=0)
+                c = jnp.concatenate([tc[I_TGT, row, :]] * (rhs // 8), 0)
+                s = jnp.concatenate([ts[I_TGT, row, :]] * (rhs // 8), 0)
+                re = jnp.where(low3, v[2 * p], sw[2 * p + 1])
+                im = jnp.where(low3, sw[2 * p], v[2 * p + 1])
                 col = pl.ds(i * T * half + p * wd, wd)
-                out[0, :, col] = jnp.where(low3, r[2 * p], rr[2 * p + 1])
-                out[1, :, col] = jnp.where(low3, rr[2 * p], r[2 * p + 1])
+                out[0, :, col] = re * c - im * s
+                out[1, :, col] = re * s + im * c
     ps_all.wait_send()
     pt_all.wait_send()
     c1_all.wait_send()
@@ -548,7 +555,7 @@
         in_specs=[pl.BlockSpec(memory_space=pltpu.HBM)] * 10,
         out_specs=pl.BlockSpec(memory_space=pltpu.VMEM),
         scratch_shapes=[vm(args[i].shape, args[i].dtype) for i in (0, 3, 4)] + [
-            vm((2,) + args[1].shape, F32), vm((3, half, half), BF16), vm((3, R, half), F32), dma((10,)),
+            vm((2,) + args[1].shape, F32), vm((3, half, half), BF16), vm((3, R, half), F32), dma((7,)),
             vm((N, 2 * wd, 2 * wd), BF16), vm((wd, 2 * wd), BF16),
             vm((wd, 2 * wd), BF16), vm((wd, 2 * wd), BF16),
             vm((ntab, R, wd), F32), vm((ntab, R, wd), F32),
@@ -557,7 +564,6 @@
             vm((S, T * rhs, wd), BF16),
             vm((S, T * rhs, 2 * wd), BF16), vm((S, T * rhs, 2 * wd), BF16),
             vm((T, S, rhs, wd), BF16), vm((T, S, rhs, wd), BF16),
-            dma(()), dma(()), dma(()), dma(()),
             dma(()), dma(()), dma(()), dma(()),
         ],
         compiler_params=pltpu.CompilerParams(

time: 15.8 us -> 15.6 us (0.987)
  Pallas kernels: 14.8 us -> 14.6 us
where the time goes in v5:
time: 15.6 us; the launch traced here: 15.4 us
  Pallas kernels  14.6 us (94%)
  local copies, waits for them, and re-layouts  0.71 us (5%)
    pallas_call x1, Pallas kernels, shards(): pl.pallas_call(functools.partial(kernel, S, T, N, src_bits, tgt_bits), ou...  14.6 us
    unnamed x1, local copies, waits for them, and re-layouts  0.71 us

profile of v5, /device:TPU:1, one launch (start us, length us, event | category | flops | bytes accessed | tf_op | source)
XLA Modules:
  0.0 15.4 jit_solution(17315155728458193941)
XLA Ops:
  0.0 14.6 %shard_map.100 = f32[2,16,2048]{2,1,0:T(8,128)S(1)} custom-call(f32[16,2048]{1,0:T(8,128)} %values_h.1, f32[16,128]{1,0:T(8,128)} %bitcast.2, bf16[64,64]{1,0:T(8,128)(2,1)} %leaf_h.1, bf16[11,2,64,64]{3,2,1,0:T(8,128)(2,1)} %lint_h.1, f32[11,3,32,64]{3,2,1,0:T(8,128)} %lphase_h.1, bf16[64,64]{1,0:T(8,128)(2,1)} %mint_h.1, f32[2,32,64]{2,1,0:T(8,128)} %mphase_h.1, ...), custom_call_target="tpu_custom_call" | custom-call | tf_op jit(solution)/shard_map/pallas_call | solution.py:552
  14.6 0.7 %copy.12 = f32[2,16,2048]{2,1,0:T(8,128)} copy(f32[2,16,2048]{2,1,0:T(8,128)S(1)} %shard_map.100) | data formatting | bytes 524288

commit v6 on v5

--- a/solution.py
+++ b/solution.py
@@ -463,8 +463,8 @@
         dst = bufs[b % 2]
         for i in range(S):
             if b == 0:
-                v = xa[i, :, :wd].astype(F32).reshape(T, rhs, wd)
-                sw = pltpu.roll(v, half, 2)
+                v = xa[i, :, :wd]
+                v, sw = (x.astype(F32).reshape(T, rhs, wd) for x in (v, pltpu.roll(v, half, 1)))
             else:
                 v, sw = split(dot(bufs[(b - 1) % 2][i], w[n - 1]))
                 dst[i, :, :wd] = rot(v, sw, 2 * n, i).astype(BF16).reshape(rows, wd)
@@ -503,8 +503,8 @@
     for blocks in groups_of(S, FIN_GROUPS):
         state = []
         for i in blocks:
-            v = recv2[:, i].astype(F32)
-            state.append((v, pltpu.roll(v, half, 2)))
+            v = recv2[:, i].reshape(rows, wd)
+            state.append(tuple(x.astype(F32).reshape(T, rhs, wd) for x in (v, pltpu.roll(v, half, 1))))
         for n in range(M, N):
             state = [step(v, sw, n, i, 2 ** (n - M)) for i, (v, sw) in zip(blocks, state)]
         state = [rot(v, sw, I_FIN, i).astype(BF16).reshape(rows, wd) for i, (v, sw) in zip(blocks, state)]

time: 15.6 us -> 15.6 us (level)
  no operation moved by 1% of the time
where the time goes in v6:
time: 15.6 us; the launch traced here: 15.4 us
  Pallas kernels  14.6 us (94%)
  local copies, waits for them, and re-layouts  0.71 us (5%)
    pallas_call x1, Pallas kernels, shards(): pl.pallas_call(functools.partial(kernel, S, T, N, src_bits, tgt_bits), ou...  14.6 us
    unnamed x1, local copies, waits for them, and re-layouts  0.71 us

profile of v6, /device:TPU:1, one launch (start us, length us, event | category | flops | bytes accessed | tf_op | source)
XLA Modules:
  0.0 15.4 jit_solution(7912646632137663300)
XLA Ops:
  0.0 14.6 %shard_map.100 = f32[2,16,2048]{2,1,0:T(8,128)S(1)} custom-call(f32[16,2048]{1,0:T(8,128)} %values_h.1, f32[16,128]{1,0:T(8,128)} %bitcast.2, bf16[64,64]{1,0:T(8,128)(2,1)} %leaf_h.1, bf16[11,2,64,64]{3,2,1,0:T(8,128)(2,1)} %lint_h.1, f32[11,3,32,64]{3,2,1,0:T(8,128)} %lphase_h.1, bf16[64,64]{1,0:T(8,128)(2,1)} %mint_h.1, f32[2,32,64]{2,1,0:T(8,128)} %mphase_h.1, ...), custom_call_target="tpu_custom_call" | custom-call | tf_op jit(solution)/shard_map/pallas_call | solution.py:552
  14.6 0.7 %copy.12 = f32[2,16,2048]{2,1,0:T(8,128)} copy(f32[2,16,2048]{2,1,0:T(8,128)S(1)} %shard_map.100) | data formatting | bytes 524288
